TPU v7x, 256 devices: a whole 4x4x8 slice. The times are simulated.
256 devices in a mesh: groups: 128 (over z, y, x), mp: 2 (over core).
Axes of the slice: x: 4, y: 4, z: 8, core: 2. Of those that a mesh axis runs over, the one named last changes fastest.
Arguments:
- latents: float32 [12288, 256], P('groups', 'mp'), may hold values from -6 to 6
- tile_slot: int32 [12288], replicated, may hold values from 0 to 12287, as said below
- live: int32 [128], replicated, may hold values from 192 to 384, as said below
- partner: int32 [128], replicated, may hold values from 0 to 127, as said below
- text_states: bfloat16 [128, 2, 154, 2432], P('groups'), may hold values from -6 to 6
- modulation: float32 [128, 2, 5, 2432], P('groups'), may hold values from -3 to 3
- w_embed: bfloat16 [64, 2432], replicated, may hold values from -0.75 to 0.75
- w_qkv: bfloat16 [2432, 3, 1280], P(None, None, 'mp'), may hold values from -0.125 to 0.125
- w_text_kv: bfloat16 [2432, 2, 1280], P(None, None, 'mp'), may hold values from -0.125 to 0.125
- w_out: bfloat16 [1280, 2432], P('mp'), may hold values from -0.15625 to 0.15625
- w_final: bfloat16 [2432, 64], replicated, may hold values from -0.125 to 0.125
- norm_gains: float32 [3, 64], replicated, may hold values from 0.5 to 24
Outputs:
- new_latents: float32 [12288, 256], P('groups', 'mp')
Inputs may be any that keep to these rules, and one draw needn't show every extreme that they name: `tile_slot`: every slot appears once; the tiles of one group go to any one group at most 2 times, and exactly 2 times for some pairs of groups. `live`: two groups that share a request hold equal counts; some group is full in every draw. partner[g] is g or g with its lowest bit flipped, and partner[partner[g]] = g; some pair shares a request in every draw.
All inputs are finite; a program needn't handle non-finite values.
Results may differ from a plain program's by a relative error of at most 0.012.
The roundings to bfloat16 on the way count: a program that leaves them out, or rounds other values in their place, can miss the bound.
Values may be sent and summed in bfloat16 or wider, within the bound.
A program may use at most 128 MiB of HBM per device.

v0:
```python
import jax
import jax.numpy as jnp
from jax import lax
from jax.sharding import PartitionSpec as P

HEAD = 64
CH = 64
TEXT = 154
ROWS = 384
TILE = 4


GUIDE = 3.5
STEP = -0.25
EPS = 1e-06


def partner_2(value, axis, apart):
    mask = 2**apart
    pairs = [(source, source ^ mask) for source in range(lax.axis_size(axis))]
    return lax.ppermute(value, axis, pairs)


def layer_norm(inputs):
    centre = jnp.mean(inputs, axis=-1, keepdims=True)
    centred = inputs - centre
    spread = jnp.mean(centred * centred, axis=-1, keepdims=True)
    return centred * lax.rsqrt(spread + EPS)


def head_norm(inputs, gains):
    square = jnp.mean(inputs * inputs, axis=-1, keepdims=True)
    return (inputs * lax.rsqrt(square + EPS) * gains).astype(jnp.bfloat16)


def exactly(left, right):
    return jnp.dot(left, right, precision=lax.Precision.HIGHEST)


def finish(residue, mixed, adaptive, w_final):
    state = residue + adaptive[:, 2, None, :] * mixed
    final = (layer_norm(state) * (1.0 + adaptive[:, 4, None, :]) + adaptive[:, 3, None, :]).astype(
        jnp.bfloat16
    )
    velocity = jnp.einsum("brd,dc->brc", final, w_final, preferred_element_type=jnp.float32)
    return velocity[1] + GUIDE * (velocity[0] - velocity[1])


def deal_tables(tile_slot, tile_count, groups_n, capacity, group_index):
    target = (tile_slot // tile_count).reshape(groups_n, tile_count)
    placed = (tile_slot % tile_count).reshape(groups_n, tile_count)
    tile_ids = jnp.arange(tile_count, dtype=jnp.int32)
    earlier = (target[:, :, None] == target[:, None, :]) & (
        tile_ids[None, None, :] < tile_ids[None, :, None]
    )
    order_rank = jnp.sum(earlier.astype(jnp.int32), axis=2)
    own_target = lax.dynamic_index_in_dim(target, group_index, 0, keepdims=False)
    own_rank = lax.dynamic_index_in_dim(order_rank, group_index, 0, keepdims=False)
    bucket_ids = jnp.arange(groups_n * capacity, dtype=jnp.int32)
    send_pos = own_target * capacity + own_rank
    sender = (bucket_ids[:, None] == send_pos[None, :]).astype(jnp.float32)
    levels = jnp.arange(capacity, dtype=jnp.int32)
    matched = (target[:, None, :] == group_index) & (
        order_rank[:, None, :] == levels[None, :, None]
    )
    position = jnp.sum(jnp.where(matched, placed[:, None, :], 0), axis=2).reshape(-1)
    present = jnp.any(matched, axis=2).reshape(-1)
    receiver = ((position[None, :] == tile_ids[:, None]) & present[None, :]).astype(jnp.float32)
    return (sender, receiver)


def shards(
    latents,
    tile_slot,
    live,
    partner,
    text_states,
    modulation,
    w_embed,
    w_qkv,
    w_text_kv,
    w_out,
    w_final,
    norm_gains,
):
    groups_n = lax.axis_size("groups")
    group_index = lax.axis_index("groups")
    member = lax.axis_index("mp")
    tile_count = ROWS // TILE
    capacity = max(2, (tile_count + groups_n - 1) // groups_n)
    narrow = latents.shape[1]
    sender, receiver = deal_tables(tile_slot, tile_count, groups_n, capacity, group_index)
    outbound = exactly(sender, latents).reshape(groups_n, capacity, narrow)
    inbound = (
        lax.all_to_all(
            outbound.astype(jnp.bfloat16), "groups", split_axis=0, concat_axis=0, tiled=True
        )
        .astype(outbound.dtype)
        .reshape(groups_n * capacity, narrow)
    )
    own_tiles = exactly(receiver, inbound)
    complete = lax.all_gather(own_tiles.astype(jnp.bfloat16), "mp", axis=1, tiled=True).astype(
        own_tiles.dtype
    )
    tokens = complete.reshape(ROWS, CH)
    hidden = jnp.dot(tokens.astype(jnp.bfloat16), w_embed, preferred_element_type=jnp.float32)
    adaptive = modulation[0]
    normed = (
        layer_norm(hidden)[None] * (1.0 + adaptive[:, 1, None, :]) + adaptive[:, 0, None, :]
    ).astype(jnp.bfloat16)
    projected = jnp.einsum("brd,dcn->brcn", normed, w_qkv, preferred_element_type=jnp.float32)
    local_width = projected.shape[-1]
    local_heads = local_width // HEAD
    projected = projected.reshape(2, ROWS, 3, local_heads, HEAD)
    query = head_norm(projected[:, :, 0], norm_gains[0])
    image_key = head_norm(projected[:, :, 1], norm_gains[1])
    image_value = projected[:, :, 2].astype(jnp.bfloat16)
    paired = jnp.stack([image_key, image_value], axis=2).reshape(2, ROWS, 2, local_width)
    mate_keys = partner_2(paired, "groups", 0).reshape(2, ROWS, 2, local_heads, HEAD)
    text_proj = jnp.einsum(
        "btd,dcn->btcn", text_states[0], w_text_kv, preferred_element_type=jnp.float32
    )
    text_proj = text_proj.reshape(2, TEXT, 2, local_heads, HEAD)
    text_key = head_norm(text_proj[:, :, 0], norm_gains[2])
    text_value = text_proj[:, :, 1].astype(jnp.bfloat16)
    mate = partner[group_index]
    joined = mate != group_index
    own_len = live[group_index]
    mate_len = jnp.where(joined, live[mate], 0)
    position = jnp.arange(ROWS, dtype=jnp.int32)
    all_keys = jnp.concatenate([text_key, image_key, mate_keys[:, :, 0]], axis=1)
    all_values = jnp.concatenate([text_value, image_value, mate_keys[:, :, 1]], axis=1)
    usable = jnp.concatenate([jnp.ones((TEXT,), bool), position < own_len, position < mate_len])

    def branch_attention(items):
        branch_query, branch_keys, branch_values = items
        scores = jnp.einsum(
            "qhe,khe->hqk", branch_query, branch_keys, preferred_element_type=jnp.float32
        ) * HEAD ** (-0.5)
        scores = jnp.where(usable[None, None, :], scores, -1e30)
        highest = jnp.max(scores, axis=-1, keepdims=True)
        raised = jnp.exp(scores - highest)
        summed = jnp.sum(raised, axis=-1, keepdims=True)
        weights = (raised / summed).astype(jnp.bfloat16)
        result_heads = jnp.einsum(
            "hqk,khe->qhe", weights, branch_values, preferred_element_type=jnp.float32
        )
        return result_heads.astype(jnp.bfloat16)

    attended = lax.map(branch_attention, (query, all_keys, all_values)).reshape(
        2, ROWS, local_width
    )
    partial_sum = jnp.einsum("brn,nd->brd", attended, w_out, preferred_element_type=jnp.float32)
    mixed = lax.psum(partial_sum.astype(jnp.bfloat16), "mp").astype(jnp.float32)
    guided = finish(hidden[None], mixed, adaptive, w_final)
    living = (position < own_len)[:, None]
    updated = tokens + STEP * jnp.where(living, guided, 0.0)
    new_tiles = updated.reshape(tile_count, TILE * CH)
    columns = lax.dynamic_slice_in_dim(new_tiles, member * narrow, narrow, 1)
    homeward = exactly(receiver.T, columns).reshape(groups_n, capacity, narrow)
    returned = (
        lax.all_to_all(
            homeward.astype(jnp.bfloat16), "groups", split_axis=0, concat_axis=0, tiled=True
        )
        .astype(homeward.dtype)
        .reshape(groups_n * capacity, narrow)
    )
    result = exactly(sender.T, returned)
    return result


def solution(mesh):
    placed = (
        P("groups", "mp"),
        P(),
        P(),
        P(),
        P("groups", None, None, None),
        P("groups", None, None, None),
        P(),
        P(None, None, "mp"),
        P(None, None, "mp"),
        P("mp", None),
        P(),
        P(),
    )
    return jax.shard_map(
        shards, mesh=mesh, in_specs=placed, out_specs=P("groups", "mp"), check_vma=False
    )
```

profile of v0, /device:TPU:1, one launch (start us, length us, event | category | flops | bytes accessed | tf_op | source)
XLA Modules:
  0.0 242.0 jit_solution(11760534496349570450)
XLA Ops:
  7.7 1.7 convert_reduce_fusion
  10.2 1.6 convolution_convert_fusion.2
  11.8 16.9 %all-to-all-start = ((bf16[128,2,128]{2,1,0:T(2,128)(2,1)}), bf16[128,2,128]{2,1,0:T(2,128)(2,1)}, u32[]{:S(2)}, u32[]{:S(2)}) async-start(bf16[128,2,128]{2,1,0:T(2,128)(2,1)} %bitcast.5), calls=%async_computation | async-start | bytes 131072 | tf_op jit(solution)/shard_map/all_to_all | solution.py:95
  31.2 16.8 %copy.51 = bf16[2432,2,640]{0,2,1:T(8,128)(2,1)} copy(bf16[2432,2,640]{2,1,0:T(2,128)(2,1)} %param.22) | data formatting | bytes 12451840 | tf_op args[8]
  49.0 2.6 %all_gather.3 = bf16[96,256]{1,0:T(8,128)(2,1)} all-gather(bf16[96,128]{1,0:T(8,128)(2,1)S(1)} %convolution_convert_fusion.3), channel_id=1, replica_groups=mesh['groups'=128,'mp'=2] {'mp'}, dimensions={1}, use_global_device_ids=true | all-gather | bytes 73728 | tf_op jit(solution)/shard_map/all_gather | solution.py:102
  55.0 10.4 %fusion.45 = f32[2,384,3,640]{1,3,2,0:T(8,128)S(1)} fusion(bf16[2432,3,640]{2,0,1:T(8,128)(2,1)} %param.21, f32[2,2432]{1,0:T(2,128)S(1)} %get-tuple-element.63, f32[2,2432]{1,0:T(2,128)S(1)} %copy-done.10, f32[384,2432]{1,0:T(8,128)S(1)} %subtract_multiply_fusion), kind=kOutput, calls=%fused_computation.29 | convolution fusion | flops 7177863168 | bytes 19011584 | tf_op jit(solution)/shard_map/brd,dcn->brcn/dot_general | solution.py:111
  70.4 5.1 %fusion.60 = f32[2,154,2,10,64]{1,4,3,2,0:T(8,128)} fusion(bf16[2,10,64,2432,1]{3,2,1,0,4:T(8,128)(2,1)S(1)} %bitcast.148, bf16[2,154,2432,1,1]{2,0,1,4,3:T(2,128)(2,1)S(1)} %bitcast.155), kind=kOutput, calls=%fused_computation.61 | convolution fusion | flops 1917583360 | bytes 9300992 | tf_op jit(solution)/shard_map/btd,dcn->btcn/dot_general | solution.py:120
  83.1 1.7 multiply_convert_fusion.2
  84.8 1.7 fusion.106
  86.5 3.8 %fusion.59 = (bf16[2,384,10,64]{1,3,2,0:T(8,128)(2,1)S(1)}, bf16[2,384,10,64]{1,3,2,0:T(8,128)(2,1)}) fusion(f32[2,384,3,10,64]{1,4,3,2,0:T(8,128)} %bitcast.145, f32[64]{0:T(128)S(1)} %get-tuple-element.68, f32[2,384,10]{1,2,0:T(8,128)S(1)} %get-tuple-element.75, f32[64]{0:T(128)S(1)} %get-tuple-element.69, f32[2,384,10]{1,2,0:T(8,128)S(1)} %get-tuple-element.74), kind=kLoop, calls=%fused_computation.57 | loop fusion | flops 2949120 | bytes 5960192 | tf_op jit(solution)/shard_map/convert_element_type | solution.py:33
  90.3 23.6 %collective-permute-done = bf16[2,384,2,640]{1,3,0,2:T(8,128)(2,1)} collective-permute-done((bf16[2,384,2,640]{1,3,0,2:T(8,128)(2,1)}, bf16[2,384,2,640]{1,3,0,2:T(8,128)(2,1)}, u32[]{:S(2)}, u32[]{:S(2)}) %collective-permute-start) | collective-permute-done | bytes 1966112 | tf_op jit(solution)/shard_map/ppermute | solution.py:21
  113.9 1.7 slice_bitcast_fusion.3
  115.7 2.8 %pad_maximum_fusion.1 = bf16[2,922,10,64]{1,3,2,0:T(8,128)(2,1)} fusion(bf16[2,384,10,64]{1,3,2,0:T(8,128)(2,1)S(1)} %get-tuple-element.56, bf16[2,384,10,64]{1,3,2,0:T(8,128)(2,1)S(1)} %get-tuple-element.54, bf16[2,154,10,64]{1,3,2,0:T(8,128)(2,1)S(1)} %multiply_convert_fusion.2), kind=kLoop, calls=%fused_computation.48 | loop fusion | flops 7080960 | bytes 4720640 | tf_op jit(solution)/shard_map/concatenate | solution.py:131
  118.5 2.8 %pad_maximum_fusion = bf16[2,922,10,64]{1,3,2,0:T(8,128)(2,1)} fusion(bf16[2,384,10,64]{1,3,2,0:T(8,128)(2,1)S(1)} %get-tuple-element.57, bf16[2,384,10,64]{1,3,2,0:T(8,128)(2,1)S(1)} %fusion.106, bf16[2,154,10,64]{1,3,2,0:T(8,128)(2,1)S(1)} %fusion.62), kind=kLoop, calls=%fused_computation.47 | loop fusion | flops 7080960 | bytes 4720640 | tf_op jit(solution)/shard_map/concatenate | solution.py:132
  121.3 34.0 %while.10 = (s32[]{:T(128)}, bf16[2,384,10,64]{1,3,2,0:T(8,128)(2,1)}, bf16[2,922,10,64]{1,3,2,0:T(8,128)(2,1)}, pred[922]{0:T(1024)(128)(4,1)S(1)}, bf16[2,384,...) while((s32[]{:T(128)}, bf16[2,384,10,64]{1,3,2,0:T(8,128)(2,1)}, ...), condition=%wide.region_11.12_spmd, body=%wide.region_8.11_spmd.sunk | while | flops 927852416 | bytes 32054248 | solution.py:150
  121.3 9.4 %fusion.122 = (f32[10,384]{1,0:T(8,128)S(1)}, f32[10,384,922]{1,2,0:T(8,128)}) fusion(pred[922]{0:T(1024)(128)(4,1)S(1)} %get-tuple-element.136, bf16[2,922,10,64]{1,3,2,0:T(8,128)(2,1)} %get-tuple-element.138, s32[]{:T(128)} %get-tuple-element.126, bf16[2,384,10,64]{1,3,2,0:T(8,128)(2,1)} %get-tuple-element.137), kind=kOutput, calls=%fused_computation.133.clone.1 | convolution fusion | flops 467344288 | bytes 15981466 | tf_op jit(solution)/shard_map/while/body/eval_jaxpr/sub | solution.py:142
  130.7 7.6 %fusion.123 = bf16[2,384,10,64]{1,3,2,0:T(8,128)(2,1)} fusion(bf16[2,384,10,64]{1,3,2,0:T(8,128)(2,1)} %get-tuple-element.127, s32[]{:T(128)} %get-tuple-element.126, f32[10,384,922]{1,2,0:T(8,128)} %get-tuple-element.117, f32[10,384]{1,0:T(8,128)S(1)} %get-tuple-element.118, bf16[2,922,10,64]{1,3,2,0:T(8,128)(2,1)} %get-tuple-element.135), kind=kOutput, calls=%fused_computation.17.clone.1 | convolution fusion | flops 460508160 | bytes 16072704 | tf_op jit(solution)/shard_map/while/body/eval_jaxpr/hqk,khe->qhe/dot_general | solution.py:145
  138.3 9.4 %fusion.122 = (f32[10,384]{1,0:T(8,128)S(1)}, f32[10,384,922]{1,2,0:T(8,128)}) fusion(pred[922]{0:T(1024)(128)(4,1)S(1)} %get-tuple-element.136, bf16[2,922,10,64]{1,3,2,0:T(8,128)(2,1)} %get-tuple-element.138, s32[]{:T(128)} %get-tuple-element.126, bf16[2,384,10,64]{1,3,2,0:T(8,128)(2,1)} %get-tuple-element.137), kind=kOutput, calls=%fused_computation.133.clone.1 | convolution fusion | flops 467344288 | bytes 15981466 | tf_op jit(solution)/shard_map/while/body/eval_jaxpr/sub | solution.py:142
  147.7 7.6 %fusion.123 = bf16[2,384,10,64]{1,3,2,0:T(8,128)(2,1)} fusion(bf16[2,384,10,64]{1,3,2,0:T(8,128)(2,1)} %get-tuple-element.127, s32[]{:T(128)} %get-tuple-element.126, f32[10,384,922]{1,2,0:T(8,128)} %get-tuple-element.117, f32[10,384]{1,0:T(8,128)S(1)} %get-tuple-element.118, bf16[2,922,10,64]{1,3,2,0:T(8,128)(2,1)} %get-tuple-element.135), kind=kOutput, calls=%fused_computation.17.clone.1 | convolution fusion | flops 460508160 | bytes 16072704 | tf_op jit(solution)/shard_map/while/body/eval_jaxpr/hqk,khe->qhe/dot_general | solution.py:145
  155.3 6.0 %convolution_convert_fusion = bf16[2,384,2432]{2,1,0:T(8,128)(2,1)} fusion(bf16[2,384,640]{1,2,0:T(8,128)(2,1)} %bitcast.156, bf16[640,2432]{1,0:T(8,128)(2,1)S(1)} %copy-done), kind=kOutput, calls=%fused_computation.37 | convolution fusion | flops 2392621056 | bytes 7831552 | tf_op jit(solution)/shard_map/brn,nd->brd/dot_general | solution.py:153
  162.7 36.1 %all-reduce.2.cloned.1.call-done = bf16[2,384,2432]{2,1,0:T(8,128)(2,1)} async-done(((bf16[2,384,2432]{2,1,0:T(8,128)(2,1)}), bf16[2,384,2432]{2,1,0:T(8,128)(2,1)}) %all-reduce.2.cloned.1.call-update) | async-done | bytes 3735568 | tf_op jit(solution)/shard_map/psum | solution.py:154
  198.7 4.4 %fusion.48 = f32[2,384]{1,0:T(2,128)S(1)} fusion(bf16[2,384,2432]{2,1,0:T(8,128)(2,1)} %all-reduce.2.cloned.1.call-done, f32[2,2432]{1,0:T(2,128)S(1)} %copy-done.7, f32[384,2432]{1,0:T(8,128)} %copy-done.1), kind=kLoop, calls=%fused_computation.35 | loop fusion | flops 7470336 | bytes 7493632 | tf_op jit(solution)/shard_map/reduce_sum | solution.py:25
  205.8 2.2 fusion.54
  209.5 24.1 %all_to_all.10 = bf16[128,2,128]{2,1,0:T(2,128)(2,1)S(1)} all-to-all(bf16[128,2,128]{2,1,0:T(2,128)(2,1)S(1)} %bitcast.151), channel_id=1, replica_groups=mesh['groups'=128,'mp'=2] {'groups'}, dimensions={0} | all-to-all | bytes 131072 | tf_op jit(solution)/shard_map/all_to_all | solution.py:162
  (99 shorter events, 25.3 us)
Async XLA Ops:
  6.5 148.8 %copy-start = (bf16[640,2432]{1,0:T(8,128)(2,1)S(1)}, bf16[640,2432]{1,0:T(8,128)(2,1)}, u32[]{:S(2)}) copy-start(bf16[640,2432]{1,0:T(8,128)(2,1)} %param.23) | copy-start | bytes 9338884
  9.6 0.6 copy-start.11
  11.8 36.1 %all-to-all-start = ((bf16[128,2,128]{2,1,0:T(2,128)(2,1)}), bf16[128,2,128]{2,1,0:T(2,128)(2,1)}, u32[]{:S(2)}, u32[]{:S(2)}) async-start(bf16[128,2,128]{2,1,0:T(2,128)(2,1)} %bitcast.5), calls=%async_computation | async-start | bytes 131072 | tf_op jit(solution)/shard_map/all_to_all | solution.py:95
  28.7 170.0 %all-reduce.2.cloned.1.call-start = ((), (), s32[]{:S(2)}) async-start(), calls=%async_computation.2 | async-start | bytes 7471104 | tf_op jit(solution)/shard_map/psum | solution.py:154
  29.4 18.6 %copy-start.12 = (s32[256]{0:T(256)}, s32[256]{0:T(256)S(1)}, u32[]{:S(2)}) copy-start(s32[256]{0:T(256)S(1)} %eq.81) | copy-start | bytes 3076
  29.7 18.3 %copy-start.13 = (pred[256]{0:T(512)(128)(4,1)}, pred[256]{0:T(512)(128)(4,1)S(1)}, u32[]{:S(2)}) copy-start(pred[256]{0:T(512)(128)(4,1)S(1)} %and.42) | copy-start | bytes 772
  31.1 16.8 %copy-start.15 = (f32[3,64]{1,0:T(4,128)S(1)}, f32[3,64]{1,0:T(4,128)}, u32[]{:S(2)}) copy-start(f32[3,64]{1,0:T(4,128)} %param.25) | copy-start | bytes 2308
  31.2 21.3 %copy-start.5 = (bf16[64,2432]{1,0:T(8,128)(2,1)S(1)}, bf16[64,2432]{1,0:T(8,128)(2,1)}, u32[]{:S(2)}) copy-start(bf16[64,2432]{1,0:T(8,128)(2,1)} %param.20) | copy-start | bytes 933892
  53.2 1.8 copy-start.1
  53.7 1.3 copy-start.10
  55.0 15.4 %slice-start = ((s8[6225920]{0:T(1024)(128)(4,1)}), s8[4194304]{0:T(1024)(128)(4,1)S(1)}, s32[]{:S(2)}) async-start(s8[6225920]{0:T(1024)(128)(4,1)} %bitcast.146), calls=%async_computation.3 | async-start | bytes 8388608
  55.0 15.4 %slice-start.1 = ((s8[6225920]{0:T(1024)(128)(4,1)}), s8[2031616]{0:T(1024)(128)(4,1)S(1)}, s32[]{:S(2)}) async-start(s8[6225920]{0:T(1024)(128)(4,1)} %bitcast.146), calls=%async_computation.4 | async-start | bytes 4063232
  65.4 2.6 %copy-start.3 = (f32[2,384,3,640]{1,3,2,0:T(8,128)}, f32[2,384,3,640]{1,3,2,0:T(8,128)S(1)}, u32[]{:S(2)}) copy-start(f32[2,384,3,640]{1,3,2,0:T(8,128)S(1)} %fusion.45) | copy-start | bytes 17694724
  66.1 4.3 %copy-start.16 = (bf16[1,2,154,2432]{3,1,2,0:T(2,128)(2,1)S(1)}, bf16[1,2,154,2432]{3,1,2,0:T(2,128)(2,1)}, u32[]{:S(2)}) copy-start(bf16[1,2,154,2432]{3,1,2,0:T(2,128)(2,1)} %param.18) | copy-start | bytes 4494340
  69.6 44.4 %collective-permute-start = (bf16[2,384,2,640]{1,3,0,2:T(8,128)(2,1)}, bf16[2,384,2,640]{1,3,0,2:T(8,128)(2,1)}, u32[]{:S(2)}, u32[]{:S(2)}) collective-permute-start(bf16[2,384,2,640]{1,3,0,2:T(8,128)(2,1)} %pad_maximum_fusion.2), channel_id=1, source_target_pairs={{0,2},{2,0},{4,6},{6,4},{8,10},{10,8},{12,14},{14,12},{16,18},{18,... | collective-permute-start | bytes 5898248 | tf_op jit(solution)/shard_map/ppermute | solution.py:21
  70.4 5.1 %copy-start.18 = (s32[128]{0:T(128)S(1)}, s32[128]{0:T(128)}, u32[]{:S(2)}) copy-start(s32[128]{0:T(128)} %param.17) | copy-start | bytes 1540
  70.4 7.9 %copy-start.14 = (s32[128]{0:T(128)S(1)}, s32[128]{0:T(128)}, u32[]{:S(2)}) copy-start(s32[128]{0:T(128)} %param.16) | copy-start | bytes 1540
  161.3 37.4 %copy-start.7 = (f32[2,2432]{1,0:T(2,128)S(1)}, f32[2,2432]{1,0:T(2,128)}, u32[]{:S(2)}) copy-start(f32[2,2432]{1,0:T(2,128)} %get-tuple-element.60) | copy-start | bytes 58372
  198.7 4.4 %copy-start.2 = (f32[384,2432]{1,0:T(8,128)S(1)}, f32[384,2432]{1,0:T(8,128)}, u32[]{:S(2)}) copy-start(f32[384,2432]{1,0:T(8,128)} %copy-done.1) | copy-start | bytes 11206660
  198.7 5.4 %copy-start.4 = (bf16[2,384,2432]{2,1,0:T(8,128)(2,1)S(1)}, bf16[2,384,2432]{2,1,0:T(8,128)(2,1)}, u32[]{:S(2)}) copy-start(bf16[2,384,2432]{2,1,0:T(8,128)(2,1)} %all-reduce.2.cloned.1.call-done) | copy-start | bytes 11206660
  204.1 1.6 copy-start.8
  204.1 1.6 copy-start.9
  204.1 1.6 copy-start.17
  205.8 2.7 %copy-start.6 = (bf16[96,256]{1,0:T(8,128)(2,1)S(1)}, bf16[96,256]{1,0:T(8,128)(2,1)}, u32[]{:S(2)}) copy-start(bf16[96,256]{1,0:T(8,128)(2,1)} %all_gather.3) | copy-start | bytes 147460
Sparse Core Ops, SparseCore 0:
  161.5 37.2 all-reduce.1
where the time goes:
time: 243 us; the launch traced here: 242 us
  matrix products  63.5 us (26%)
  waiting for transfers between devices  59.7 us (25%)
  local copies, waits for them, and re-layouts  29.9 us (12%)
  other arithmetic  27.7 us (11%)
  blocking collectives  26.7 us (11%)
  starting transfers between devices  17.7 us (7%)
  between operations  16.7 us (7%)
    psum x1, waiting for transfers between devices, shards(): mixed = lax.psum(partial_sum.astype(jnp.bfloat16), 'mp').astype(jnp.float32)  36.1 us
    all_to_all x1, blocking collectives, shards(): lax.all_to_all(homeward.astype(jnp.bfloat16), 'groups', split_axis=0, con...  24.1 us
    ppermute x1, waiting for transfers between devices, partner_2(): return lax.ppermute(value, axis, pairs)  23.6 us
    unnamed x44, local copies, waits for them, and re-layouts  21.3 us
    sub x2, matrix products, branch_attention(): raised = jnp.exp(scores - highest)  18.8 us
    all_to_all x1, starting transfers between devices, shards(): lax.all_to_all(outbound.astype(jnp.bfloat16), 'groups', split_axis=0, con...  16.9 us
    dot_general x2, matrix products, branch_attention(): jnp.einsum('hqk,khe->qhe', weights, branch_values, preferred_element_type...  15.2 us
    dot_general x1, matrix products, shards(): jnp.einsum('brd,dcn->brcn', normed, w_qkv, preferred_element_type=jnp.flo...  10.4 us
  transfers between devices with their start and end apart: 3, of which 2 were waited for; matrix products, arithmetic and copies ran while one was open for 15% of the time, Pallas kernels for 0%

commit v1 on v0

v1 whole, which is shorter than its diff:
```python
import functools
import jax
import jax.numpy as jnp
from jax import lax
from jax.experimental import pallas as pl
from jax.experimental.pallas import tpu as pltpu
from jax.sharding import PartitionSpec as P

HEAD = 64
CH = 64
TEXT = 154
ROWS = 384
TILE = 4
TILES = 96
D = 2432
Z = 8
XY = 16
HALF = ROWS // 2

GUIDE = 3.5
STEP = -0.25
EPS = 1e-06
F32 = jnp.float32
BF16 = jnp.bfloat16
MESH = pl.DeviceIdType.MESH
VMEM = pl.BlockSpec(memory_space=pltpu.VMEM)
SMEM = pl.BlockSpec(memory_space=pltpu.SMEM)


def iota(shape, axis):
    return lax.broadcasted_iota(jnp.int32, shape, axis)


def onehot(condition):
    return jnp.where(condition, 1.0, 0.0).astype(BF16)


def group_of(slot):
    return (slot * 43691) >> 22


def where_am_i():
    group = lax.axis_index("groups")
    return group, lax.axis_index("mp"), lax.div(group, XY), lax.rem(group, XY)


def z_peer(z, k):
    return lax.rem(z + k, Z)


def my_buckets_row(slot_ref, group):
    mine = jnp.broadcast_to(group_of(slot_ref[pl.ds(group, 1), :]).astype(F32), (TILES, TILES))
    across, down = iota((TILES, TILES), 1), iota((TILES, TILES), 0)
    column = jnp.sum(jnp.where(across == down, mine, 0.0), axis=1, keepdims=True)
    earlier = jnp.where((mine == column) & (down < across), 1.0, 0.0)
    return 2.0 * mine[:1] + jnp.sum(earlier, axis=0, keepdims=True)


def my_buckets_column(slot_ref, group):
    mine = jnp.broadcast_to(group_of(slot_ref[pl.ds(group, 1), :]).astype(F32), (TILES, TILES))
    across, down = iota((TILES, TILES), 1), iota((TILES, TILES), 0)
    column = jnp.sum(jnp.where(across == down, mine, 0.0), axis=1, keepdims=True)
    earlier = jnp.where((mine == column) & (across < down), 1.0, 0.0)
    return 2.0 * column + jnp.sum(earlier, axis=1, keepdims=True)


def landing(slot_ref, rows, source, wanted, rank_wanted):
    slot = slot_ref[...]
    target = group_of(slot)
    placed = slot - target * TILES
    pick = onehot(iota((rows, Z * XY), 1) == source)
    goal = jnp.dot(pick, target.astype(F32).astype(BF16), preferred_element_type=F32)
    place = jnp.dot(pick, placed.astype(F32).astype(BF16), preferred_element_type=F32)
    matched = jnp.where(goal == wanted, 1.0, 0.0)
    before = onehot(iota((TILES, TILES), 0) < iota((TILES, TILES), 1))
    rank = jnp.dot(matched.astype(BF16), before, preferred_element_type=F32)
    return jnp.where((matched > 0.5) & (rank == rank_wanted), place + 1.0, 0.0)


def deal_kernel(
    lat_ref, slot_ref, mod_ref, own_ref, par_ref, modp_ref,
    buf_s, buf_a, buf_b, buf_c, mod_s, ssem_a, rsem_a, ssem_b, rsem_b, msem,
):
    group, core, z, xy = where_am_i()
    me = xy * 2 + core
    mate = group + 1 - 2 * lax.rem(group, 2)
    barrier = pltpu.get_barrier_semaphore()

    def z_id(k):
        return {"groups": z_peer(z, k) * XY + xy, "mp": core}

    def plane(k):
        t = lax.rem(me + k, 2 * XY)
        return lax.div(t, 2), lax.rem(t, 2)

    def plane_id(k):
        at, other = plane(k)
        return {"groups": z * XY + at, "mp": other}

    @pl.loop(1, Z)
    def _(k):
        pl.semaphore_signal(barrier, inc=1, device_id=z_id(k), device_id_type=MESH)

    @pl.loop(1, 2 * XY)
    def _(k):
        pl.semaphore_signal(barrier, inc=1, device_id=plane_id(k), device_id_type=MESH)

    sender = onehot(iota((256, TILES), 0).astype(F32) == my_buckets_row(slot_ref, group))
    buf_s[...] = (
        jnp.dot(sender, lat_ref[...].astype(BF16), preferred_element_type=F32)
        .astype(BF16).reshape(Z, 32, 128)
    )
    pl.semaphore_wait(barrier, Z - 1 + 2 * XY - 1)

    def send_a(k):
        return pltpu.make_async_remote_copy(
            src_ref=buf_s.at[z_peer(z, k)], dst_ref=buf_a.at[z],
            send_sem=ssem_a.at[k], recv_sem=rsem_a.at[z],
            device_id=z_id(k), device_id_type=MESH,
        )

    def come_a(k):
        other = z_peer(z, k)
        return pltpu.make_async_remote_copy(
            src_ref=buf_s.at[other], dst_ref=buf_a.at[other],
            send_sem=ssem_a.at[k], recv_sem=rsem_a.at[other],
            device_id=z_id(k), device_id_type=MESH,
        )

    @pl.loop(1, Z)
    def _(k):
        send_a(k).start()

    mod_copy = pltpu.make_async_remote_copy(
        src_ref=mod_ref.at[pl.ds(0, 2)], dst_ref=mod_s,
        send_sem=msem.at[0], recv_sem=msem.at[1],
        device_id={"groups": mate, "mp": core}, device_id_type=MESH,
    )
    mod_copy.start()
    buf_a[z] = buf_s[z]

    row = iota((512, 1), 0)
    low = group - lax.rem(group, 2)
    brought = landing(
        slot_ref, 512, (row & 7) * XY + (row >> 5),
        (low + ((row >> 4) & 1)).astype(F32), ((row >> 3) & 1).astype(F32),
    )
    spot = lax.dot_general(
        jnp.ones((8, TILES), BF16), brought.astype(BF16), (((1,), (1,)), ((), ())),
        preferred_element_type=F32,
    )[:1]
    hit = iota((TILES, 512), 0).astype(F32) + 1.0 == spot
    member = (iota((TILES, 512), 1) >> 4) & 1
    bit = lax.rem(group, 2)
    take_own = onehot(hit & (member == bit))
    take_par = onehot(hit & (member != bit))
    out_row = iota((256, 256), 0)
    reorder = onehot(
        iota((256, 256), 1) == (out_row & 7) * 32 + (out_row >> 4) * 2 + ((out_row >> 3) & 1)
    )

    @pl.loop(1, Z)
    def _(k):
        come_a(k).wait_recv()

    buf_b[...] = (
        jnp.dot(reorder, buf_a[...].reshape(256, 128), preferred_element_type=F32)
        .astype(BF16).reshape(Z, 32, 128)
    )

    def send_b(k):
        at, other = plane(k)
        return pltpu.make_async_remote_copy(
            src_ref=buf_b.at[lax.div(at, 2)], dst_ref=buf_c.at[core, xy],
            send_sem=ssem_b.at[k], recv_sem=rsem_b.at[me],
            device_id=plane_id(k), device_id_type=MESH,
        )

    def come_b(k):
        at, other = plane(k)
        return pltpu.make_async_remote_copy(
            src_ref=buf_b.at[lax.div(at, 2)], dst_ref=buf_c.at[other, at],
            send_sem=ssem_b.at[k], recv_sem=rsem_b.at[at * 2 + other],
            device_id=plane_id(k), device_id_type=MESH,
        )

    @pl.loop(1, 2 * XY)
    def _(k):
        send_b(k).start()

    buf_c[core, xy] = buf_b[lax.div(xy, 2)]

    @pl.loop(1, 2 * XY)
    def _(k):
        come_b(k).wait_recv()

    for half in range(2):
        landed = buf_c[half].reshape(512, 128)
        for take, out in ((take_own, own_ref), (take_par, par_ref)):
            tiles = jnp.dot(take, landed, preferred_element_type=F32).astype(BF16)
            out[2 * half] = tiles[:, :CH]
            out[2 * half + 1] = tiles[:, CH:]

    mod_copy.wait_recv()
    modp_ref[...] = mod_s[...]

    @pl.loop(1, Z)
    def _(k):
        send_a(k).wait_send()

    @pl.loop(1, 2 * XY)
    def _(k):
        send_b(k).wait_send()

    mod_copy.wait_send()


def deal(latents, slots, mod):
    return pl.pallas_call(
        deal_kernel,
        out_shape=(
            jax.ShapeDtypeStruct((TILE, TILES, CH), BF16),
            jax.ShapeDtypeStruct((TILE, TILES, CH), BF16),
            jax.ShapeDtypeStruct((2, 2, D), F32),
        ),
        in_specs=[VMEM] * 3,
        out_specs=(VMEM,) * 3,
        scratch_shapes=[
            pltpu.VMEM((Z, 32, 128), BF16),
            pltpu.VMEM((Z, 32, 128), BF16),
            pltpu.VMEM((Z, 32, 128), BF16),
            pltpu.VMEM((2, XY, 32, 128), BF16),
            pltpu.VMEM((2, 2, D), F32),
            pltpu.SemaphoreType.DMA((Z,)),
            pltpu.SemaphoreType.DMA((Z,)),
            pltpu.SemaphoreType.DMA((2 * XY,)),
            pltpu.SemaphoreType.DMA((2 * XY,)),
            pltpu.SemaphoreType.DMA((2,)),
        ],
        compiler_params=pltpu.CompilerParams(collective_id=0, has_side_effects=True),
        name="deal",
    )(latents, slots, mod)


CHUNKS = ((0, 512), (512, 512), (1024, 512), (1536, 512), (2048, 384))


def home_kernel(
    att_ref, wout_ref, tok_ref, wemb_ref, wfin_ref, mod_ref, live_ref, lat_ref, slot_ref, out_ref,
    give, got, kept, hid, vel, buf_d, buf_e, buf_f, buf_g, xsend, xrecv, ssem_b, rsem_b, ssem_a, rsem_a,
):
    group, core, z, xy = where_am_i()
    other = 1 - core
    barrier = pltpu.get_barrier_semaphore()

    def z_id(k):
        return {"groups": z_peer(z, k) * XY + xy, "mp": core}

    def plane(k):
        return lax.rem(xy + k, XY)

    def plane_id(k):
        return {"groups": z * XY + plane(k), "mp": core}

    sibling = {"groups": group, "mp": other}
    pl.semaphore_signal(barrier, inc=1, device_id=sibling, device_id_type=MESH)

    @pl.loop(1, Z)
    def _(k):
        pl.semaphore_signal(barrier, inc=1, device_id=z_id(k), device_id_type=MESH)

    @pl.loop(1, XY)
    def _(k):
        pl.semaphore_signal(barrier, inc=1, device_id=plane_id(k), device_id_type=MESH)

    def exchange(b):
        return pltpu.make_async_remote_copy(
            src_ref=give.at[b], dst_ref=got.at[b], send_sem=xsend.at[b], recv_sem=xrecv.at[b],
            device_id=sibling, device_id_type=MESH,
        )

    def project(b, half, dst):
        rows = att_ref[b, half]
        for start, size in CHUNKS:
            dst[b, :, start:start + size] = jnp.dot(
                rows, wout_ref[:, start:start + size], preferred_element_type=F32
            ).astype(BF16)

    for b in range(2):
        project(b, other, give)
        if b == 0:
            pl.semaphore_wait(barrier, 1 + Z - 1 + XY - 1)
        exchange(b).start()
    for b in range(2):
        project(b, core, kept)
    for start, size in CHUNKS:
        hid[:, start:start + size] = jnp.dot(
            tok_ref[core], wemb_ref[:, start:start + size], preferred_element_type=F32
        )

    block = 48
    for b in range(2):
        exchange(b).wait_recv()
        gate, shift, scale = (mod_ref[i, b:b + 1, :] for i in (2, 3, 4))

        @pl.loop(0, HALF // block)
        def _(i):
            rows = pl.ds(pl.multiple_of(i * block, block), block)
            mixed = kept[b, rows, :].astype(F32) + got[b, rows, :].astype(F32)
            state = hid[rows, :] + gate * mixed
            centred = state - jnp.mean(state, axis=-1, keepdims=True)
            spread = jnp.mean(centred * centred, axis=-1, keepdims=True)
            final = (centred * lax.rsqrt(spread + EPS) * (1.0 + scale) + shift).astype(BF16)
            vel[b, rows, :] = lax.dot_general(
                final, wfin_ref[...], (((1,), (1,)), ((), ())), preferred_element_type=F32
            )

    guided = vel[1] + GUIDE * (vel[0] - vel[1])
    row = iota((HALF, CH), 0)
    upper = jnp.where(row >= TILES, 1, 0)
    position = (row - upper * TILES) * TILE + 2 * core + upper
    change = jnp.where(position < live_ref[group], STEP * guided, 0.0)
    change = jnp.concatenate([change[:TILES], change[TILES:]], axis=1).astype(BF16)

    row = iota((256, 1), 0)
    brought = landing(
        slot_ref, 256, (row & 7) * XY + (row >> 4), group.astype(F32), ((row >> 3) & 1).astype(F32)
    )
    spot = jnp.sum(brought, axis=1, keepdims=True)
    back = onehot(spot == iota((256, TILES), 1).astype(F32) + 1.0)
    buf_d[...] = (
        jnp.dot(back, change, preferred_element_type=F32).astype(BF16).reshape(XY, 16, 128)
    )

    def send_b(k):
        return pltpu.make_async_remote_copy(
            src_ref=buf_d.at[plane(k)], dst_ref=buf_e.at[xy],
            send_sem=ssem_b.at[k], recv_sem=rsem_b.at[xy],
            device_id=plane_id(k), device_id_type=MESH,
        )

    def come_b(k):
        return pltpu.make_async_remote_copy(
            src_ref=buf_d.at[plane(k)], dst_ref=buf_e.at[plane(k)],
            send_sem=ssem_b.at[k], recv_sem=rsem_b.at[plane(k)],
            device_id=plane_id(k), device_id_type=MESH,
        )

    @pl.loop(1, XY)
    def _(k):
        send_b(k).start()

    buf_e[xy] = buf_d[xy]
    out_row = iota((256, 256), 0)
    reorder = onehot(
        iota((256, 256), 1) == ((out_row >> 1) & 15) * 16 + (out_row & 1) * 8 + (out_row >> 5)
    )
    gather = onehot(iota((TILES, 256), 1).astype(F32) == my_buckets_column(slot_ref, group))

    @pl.loop(1, XY)
    def _(k):
        come_b(k).wait_recv()

    buf_f[...] = (
        jnp.dot(reorder, buf_e[...].reshape(256, 128), preferred_element_type=F32)
        .astype(BF16).reshape(Z, 32, 128)
    )

    def send_a(k):
        return pltpu.make_async_remote_copy(
            src_ref=buf_f.at[z_peer(z, k)], dst_ref=buf_g.at[z],
            send_sem=ssem_a.at[k], recv_sem=rsem_a.at[z],
            device_id=z_id(k), device_id_type=MESH,
        )

    def come_a(k):
        return pltpu.make_async_remote_copy(
            src_ref=buf_f.at[z_peer(z, k)], dst_ref=buf_g.at[z_peer(z, k)],
            send_sem=ssem_a.at[k], recv_sem=rsem_a.at[z_peer(z, k)],
            device_id=z_id(k), device_id_type=MESH,
        )

    @pl.loop(1, Z)
    def _(k):
        send_a(k).start()

    buf_g[z] = buf_f[z]

    @pl.loop(1, Z)
    def _(k):
        come_a(k).wait_recv()

    out_ref[...] = lat_ref[...] + jnp.dot(
        gather, buf_g[...].reshape(256, 128), preferred_element_type=F32
    )

    for b in range(2):
        exchange(b).wait_send()

    @pl.loop(1, XY)
    def _(k):
        send_b(k).wait_send()

    @pl.loop(1, Z)
    def _(k):
        send_a(k).wait_send()


def home(attended, w_out, tokens, w_embed, w_final, mod, live, latents, slots):
    return pl.pallas_call(
        home_kernel,
        out_shape=jax.ShapeDtypeStruct((TILES, 128), F32),
        in_specs=[VMEM] * 6 + [SMEM] + [VMEM] * 2,
        out_specs=VMEM,
        scratch_shapes=[
            pltpu.VMEM((2, HALF, D), BF16),
            pltpu.VMEM((2, HALF, D), BF16),
            pltpu.VMEM((2, HALF, D), BF16),
            pltpu.VMEM((HALF, D), F32),
            pltpu.VMEM((2, HALF, CH), F32),
            pltpu.VMEM((XY, 16, 128), BF16),
            pltpu.VMEM((XY, 16, 128), BF16),
            pltpu.VMEM((Z, 32, 128), BF16),
            pltpu.VMEM((Z, 32, 128), BF16),
            pltpu.SemaphoreType.DMA((2,)),
            pltpu.SemaphoreType.DMA((2,)),
            pltpu.SemaphoreType.DMA((XY,)),
            pltpu.SemaphoreType.DMA((XY,)),
            pltpu.SemaphoreType.DMA((Z,)),
            pltpu.SemaphoreType.DMA((Z,)),
        ],
        compiler_params=pltpu.CompilerParams(
            collective_id=1, has_side_effects=True, vmem_limit_bytes=40 << 20
        ),
        name="home",
    )(attended, w_out, tokens, w_embed, w_final, mod, live, latents, slots)


def layer_norm(inputs):
    centre = jnp.mean(inputs, axis=-1, keepdims=True)
    centred = inputs - centre
    spread = jnp.mean(centred * centred, axis=-1, keepdims=True)
    return centred * lax.rsqrt(spread + EPS)


def head_norm(inputs, gains):
    square = jnp.mean(inputs * inputs, axis=-1, keepdims=True)
    return (inputs * lax.rsqrt(square + EPS) * gains).astype(BF16)


def shards(
    latents, tile_slot, live, partner, text_states, modulation,
    w_embed, w_qkv, w_text_kv, w_out, w_final, norm_gains,
):
    group = lax.axis_index("groups")
    slots = tile_slot.reshape(Z * XY, TILES)
    mod = modulation[0].transpose(1, 0, 2)
    own, par, mod_par = deal(latents, slots, mod)
    tokens = jnp.concatenate([own.reshape(ROWS, CH), par.reshape(ROWS, CH)], axis=0)
    hidden = jnp.dot(tokens, w_embed, preferred_element_type=F32)
    scaled = layer_norm(hidden).reshape(2, 1, ROWS, D)
    mods = jnp.stack([mod[:2], mod_par])
    normed = (scaled * (1.0 + mods[:, 1, :, None, :]) + mods[:, 0, :, None, :]).astype(BF16)
    w3 = w_qkv.transpose(1, 0, 2)
    local_heads = w_qkv.shape[2] // HEAD
    query = jnp.dot(normed[0].reshape(2 * ROWS, D), w3[0], preferred_element_type=F32)
    keys = jnp.dot(normed.reshape(4 * ROWS, D), w3[1], preferred_element_type=F32)
    values = jnp.dot(normed.reshape(4 * ROWS, D), w3[2], preferred_element_type=F32)
    query = head_norm(query.reshape(2, ROWS, local_heads, HEAD), norm_gains[0])
    keys = head_norm(keys.reshape(2, 2, ROWS, local_heads, HEAD), norm_gains[1])
    values = values.reshape(2, 2, ROWS, local_heads, HEAD).astype(BF16)
    text_proj = jnp.einsum("btd,dcn->btcn", text_states[0], w_text_kv, preferred_element_type=F32)
    text_proj = text_proj.reshape(2, TEXT, 2, local_heads, HEAD)
    text_key = head_norm(text_proj[:, :, 0], norm_gains[2])
    text_value = text_proj[:, :, 1].astype(BF16)
    mate = partner[group]
    own_len = live[group]
    mate_len = jnp.where(mate != group, live[mate], 0)
    order = jnp.arange(ROWS, dtype=jnp.int32)
    position = (order % TILES) * TILE + order // TILES
    all_keys = jnp.concatenate([text_key, keys[0], keys[1]], axis=1)
    all_values = jnp.concatenate([text_value, values[0], values[1]], axis=1)
    usable = jnp.concatenate([jnp.ones((TEXT,), bool), position < own_len, position < mate_len])

    def branch_attention(items):
        branch_query, branch_keys, branch_values = items
        scores = jnp.einsum(
            "qhe,khe->hqk", branch_query, branch_keys, preferred_element_type=F32
        ) * HEAD ** (-0.5)
        scores = jnp.where(usable[None, None, :], scores, -1e30)
        highest = jnp.max(scores, axis=-1, keepdims=True)
        raised = jnp.exp(scores - highest)
        summed = jnp.sum(raised, axis=-1, keepdims=True)
        weights = (raised / summed).astype(BF16)
        result_heads = jnp.einsum(
            "hqk,khe->qhe", weights, branch_values, preferred_element_type=F32
        )
        return result_heads.astype(BF16)

    attended = lax.map(branch_attention, (query, all_keys, all_values))
    return home(
        attended.reshape(2, 2, HALF, local_heads * HEAD), w_out, own.reshape(2, HALF, CH),
        w_embed, w_final.T, mod, live, latents, slots,
    )


def solution(mesh):
    placed = (
        P("groups", "mp"), P(), P(), P(),
        P("groups", None, None, None), P("groups", None, None, None),
        P(), P(None, None, "mp"), P(None, None, "mp"), P("mp", None), P(), P(),
    )
    return jax.shard_map(
        shards, mesh=mesh, in_specs=placed, out_specs=P("groups", "mp"), check_vma=False
    )
```

time: 243 us -> 186 us (0.77)
  waiting for transfers between devices: 59.7 us -> 0 us
  Pallas kernels: 0 us -> 45 us
  blocking collectives: 26.7 us -> 0 us
  local copies, waits for them, and re-layouts: 29.9 us -> 50.7 us
  starting transfers between devices: 17.7 us -> 0 us
  between operations: 16.7 us -> 3.17 us
  other arithmetic: 27.7 us -> 20.9 us
    pallas_call x0 -> x2, Pallas kernels: none -> 45 us  [the longest x1 23.7 us: deal(): pl.pallas_call(deal_kernel, out_shape=(jax.ShapeDtypeStruct((TILE, TILES,...]
    psum x1 -> x0, waiting for transfers between devices: 36.1 us -> none  [shards(): mixed = lax.psum(partial_sum.astype(jnp.bfloat16), 'mp').astype(jnp.float32)]
    all_to_all x1 -> x0, blocking collectives: 24.1 us -> none  [shards(): lax.all_to_all(homeward.astype(jnp.bfloat16), 'groups', split_axis=0, con...]
    ppermute x1 -> x0, waiting for transfers between devices: 23.6 us -> none  [partner_2(): return lax.ppermute(value, axis, pairs)]
    dot_general x0 -> x4, local copies, waits for them, and re-layouts: none -> 20.5 us  [the longest x2 11.4 us: shards(): jnp.dot(normed.reshape(4 * ROWS, D), w3[1], preferred_element_type=F32)]
    all_to_all x1 -> x0, starting transfers between devices: 16.9 us -> none  [shards(): lax.all_to_all(outbound.astype(jnp.bfloat16), 'groups', split_axis=0, con...]
    reduce_sum x3 -> x0, other arithmetic: 6.12 us -> none  [the longest x1 4.38 us: layer_norm(): centre = jnp.mean(inputs, axis=-1, keepdims=True)]
    reshape x2 -> x3, local copies, waits for them, and re-layouts: 0.16 us -> 6.18 us  [the longest x2 4.69 us: shards(): attended.reshape(2, 2, HALF, local_heads * HEAD)]
  transfers between devices with their start and end apart: 3 -> 0, of which waited for: 2 -> 0; matrix products, arithmetic and copies ran while one was open for 15% -> 0% of each run, Pallas kernels for 0% -> 0%
where the time goes in v1:
time: 186 us; the launch traced here: 185 us
  matrix products  64.8 us (35%)
  local copies, waits for them, and re-layouts  50.7 us (27%)
  Pallas kernels  45 us (24%)
  other arithmetic  20.9 us (11%)
  between operations  3.17 us (2%)
    pallas_call x1, Pallas kernels, deal(): pl.pallas_call(deal_kernel, out_shape=(jax.ShapeDtypeStruct((TILE, TILES,...  23.7 us
    pallas_call x1, Pallas kernels, home(): pl.pallas_call(home_kernel, out_shape=jax.ShapeDtypeStruct((TILES, 128),...  21.3 us
    unnamed x28, local copies, waits for them, and re-layouts  20.1 us
    sub x2, matrix products, branch_attention(): raised = jnp.exp(scores - highest)  19.1 us
    dot_general x2, matrix products, branch_attention(): jnp.einsum('hqk,khe->qhe', weights, branch_values, preferred_element_type...  14.5 us
    dot_general x2, local copies, waits for them, and re-layouts, shards(): jnp.dot(normed.reshape(4 * ROWS, D), w3[1], preferred_element_type=F32)  11.4 us
    dot_general x1, matrix products, shards(): jnp.dot(normed.reshape(4 * ROWS, D), w3[1], preferred_element_type=F32)  8.59 us
    dot_general x1, matrix products, shards(): jnp.dot(normed.reshape(4 * ROWS, D), w3[2], preferred_element_type=F32)  8.5 us

profile of v1, /device:TPU:1, one launch (start us, length us, event | category | flops | bytes accessed | tf_op | source)
XLA Modules:
  0.0 184.6 jit_solution(6429655128231192520)
XLA Ops:
  0.0 1.5 reshape.87.slot_ref
  1.5 23.7 %deal.1 = (bf16[4,96,64]{2,1,0:T(8,128)(2,1)}, bf16[4,96,64]{2,1,0:T(8,128)(2,1)}, f32[2,2,2432]{2,1,0:T(2,128)}) custom-call(f32[96,128]{1,0:T(8,128)} %lat_ref.3, s32[128,96]{1,0:T(8,128)} %reshape.87.slot_ref, f32[5,2,2432]{2,1,0:T(2,128)} %bitcast.149), custom_call_target="tpu_custom_call" | custom-call | tf_op jit(solution)/shard_map/deal/pallas_call | solution.py:219
  25.2 2.3 %fusion.84 = (f32[768]{0:T(1024)S(1)}, f32[768,2432]{1,0:T(8,128)S(1)}) fusion(bf16[64,2432]{1,0:T(8,128)(2,1)} %wemb_ref.1, bf16[384,64]{1,0:T(8,128)(2,1)} %bitcast.161, bf16[384,64]{1,0:T(8,128)(2,1)} %bitcast.152), kind=kOutput, calls=%fused_computation.98 | convolution fusion | flops 241138944 | bytes 7883776 | tf_op jit(solution)/shard_map/dot_general | solution.py:460
  28.4 3.8 %subtract_multiply_fusion = f32[768,2432]{1,0:T(8,128)} fusion(f32[768,2432]{1,0:T(8,128)S(1)} %get-tuple-element.73, f32[768]{0:T(1024)S(1)} %add_rsqrt_fusion.3, f32[768]{0:T(1024)S(1)} %broadcast_multiply_fusion), kind=kLoop, calls=%fused_computation.35 | loop fusion | flops 3735552 | bytes 14948352 | tf_op jit(solution)/shard_map/mul | solution.py:443
  33.0 7.7 %add_convert_fusion = bf16[2,2,384,2432]{3,2,1,0:T(8,128)(2,1)} fusion(f32[2,2,2432]{2,1,0:T(2,128)S(1)} %get-tuple-element.66, f32[2,2,2432]{2,1,0:T(2,128)S(1)} %get-tuple-element.65, f32[2,384,2432]{2,1,0:T(8,128)} %bitcast.155), kind=kLoop, calls=%fused_computation.29 | loop fusion | flops 11206656 | bytes 15020032 | tf_op jit(solution)/shard_map/convert_element_type | solution.py:463
  40.7 5.8 %slice_bitcast_fusion.2 = (bf16[640,2432]{0,1:T(8,128)(2,1)}, bf16[640,2432]{0,1:T(8,128)(2,1)}, bf16[640,2432]{0,1:T(8,128)(2,1)S(1)}) fusion(bf16[3,2432,640]{2,1,0:T(8,128)(2,1)} %bitcast.156), kind=kLoop, calls=%fused_computation.40 | loop fusion | bytes 18677760 | tf_op jit(solution)/shard_map/dot_general | solution.py:467
  46.6 5.5 %copy.22 = bf16[640,2432]{1,0:T(8,128)(2,1)} copy(bf16[640,2432]{0,1:T(8,128)(2,1)} %get-tuple-element.59) | data formatting | bytes 6225920 | tf_op jit(solution)/shard_map/dot_general | solution.py:466
  52.1 5.8 %multiply_reduce_fusion.2 = (f32[2,384,10]{1,2,0:T(8,128)S(1)}, f32[2,384,10,64]{1,3,2,0:T(8,128)S(1)}) fusion(bf16[10,64,2432,1]{2,1,0,3:T(8,128)(2,1)} %bitcast.158, bf16[2,2,384,2432]{3,2,1,0:T(8,128)(2,1)} %add_convert_fusion), kind=kOutput, calls=%fused_computation.46 | convolution fusion | flops 2391728640 | bytes 8845312 | tf_op jit(solution)/shard_map/dot_general | solution.py:466
  59.3 5.5 %copy.23 = bf16[640,2432]{1,0:T(8,128)(2,1)} copy(bf16[640,2432]{0,1:T(8,128)(2,1)} %get-tuple-element.58) | data formatting | bytes 6225920 | tf_op jit(solution)/shard_map/dot_general | solution.py:467
  64.8 8.6 %multiply_reduce_fusion.1 = (f32[2,2,384,10]{2,3,1,0:T(8,128)S(1)}, f32[2,2,384,10,64]{2,4,3,1,0:T(8,128)S(1)}) fusion(bf16[10,64,2432,1,1]{2,1,0,4,3:T(8,128)(2,1)} %bitcast.159, bf16[2,2,384,2432]{3,2,1,0:T(8,128)(2,1)} %add_convert_fusion), kind=kOutput, calls=%fused_computation.37 | convolution fusion | flops 4783457280 | bytes 14577664 | tf_op jit(solution)/shard_map/dot_general | solution.py:467
  74.4 1.5 slice_bitcast_fusion.7
  75.9 3.6 %copy.21 = bf16[640,2432]{1,0:T(8,128)(2,1)} copy(bf16[640,2432]{0,1:T(8,128)(2,1)S(1)} %get-tuple-element.60) | data formatting | bytes 6225920 | tf_op jit(solution)/shard_map/dot_general | solution.py:468
  79.6 8.5 %fusion.50 = bf16[2,2,384,10,64]{2,4,3,1,0:T(8,128)(2,1)S(1)} fusion(bf16[10,64,2432,1,1]{2,1,0,4,3:T(8,128)(2,1)} %bitcast.160, bf16[2,2,384,2432]{3,2,1,0:T(8,128)(2,1)} %add_convert_fusion), kind=kOutput, calls=%fused_computation.47 | convolution fusion | flops 4782489600 | bytes 12550144 | tf_op jit(solution)/shard_map/dot_general | solution.py:468
  88.3 16.8 %copy.19 = bf16[2432,2,640]{0,2,1:T(8,128)(2,1)} copy(bf16[2432,2,640]{2,1,0:T(2,128)(2,1)} %param.22) | data formatting | bytes 12451840 | tf_op args[8]
  105.1 6.2 %fusion.53 = f32[2,154,2,10,64]{1,4,3,2,0:T(8,128)S(1)} fusion(bf16[2,10,64,2432,1]{3,2,1,0,4:T(8,128)(2,1)} %bitcast.157, bf16[2,154,2432,1,1]{2,0,1,4,3:T(2,128)(2,1)} %bitcast.163), kind=kOutput, calls=%fused_computation.48 | convolution fusion | flops 1917583360 | bytes 9300992 | tf_op jit(solution)/shard_map/btd,dcn->btcn/dot_general | solution.py:472
  112.7 4.8 %pad_maximum_fusion = (bf16[2,922,10,64]{1,3,2,0:T(8,128)(2,1)}, bf16[2,922,10,64]{1,3,2,0:T(8,128)(2,1)}) fusion(bf16[2,384,10,64]{1,3,2,0:T(8,128)(2,1)S(1)} %get-tuple-element.64, bf16[2,384,10,64]{1,3,2,0:T(8,128)(2,1)S(1)} %get-tuple-element.63, bf16[2,154,10,64]{1,3,2,0:T(8,128)(2,1)S(1)} %fusion.55, bf16[2,384,10,64]{1,3,2,0:T(8,128)(2,1)S(1)} %copy-done.9, ...), kind=kLoop, calls=%fused_computation.43 | loop fusion | flops 14161920 | bytes 9441280 | tf_op jit(solution)/shard_map/concatenate | solution.py:482
  122.4 33.5 %while.10 = (s32[]{:T(128)}, bf16[2,384,10,64]{1,3,2,0:T(8,128)(2,1)}, bf16[2,922,10,64]{1,3,2,0:T(8,128)(2,1)}, pred[922]{0:T(1024)(128)(4,1)S(1)}, bf16[2,384,...) while((s32[]{:T(128)}, bf16[2,384,10,64]{1,3,2,0:T(8,128)(2,1)}, ...), condition=%wide.region_8.9_spmd, body=%wide.region_5.8_spmd.sunk | while | flops 927852416 | bytes 41504768 | solution.py:500
  122.4 9.5 %fusion.98 = (f32[10,384]{1,0:T(8,128)S(1)}, f32[10,384,922]{1,2,0:T(8,128)}) fusion(pred[922]{0:T(1024)(128)(4,1)S(1)} %get-tuple-element.140, bf16[2,922,10,64]{1,3,2,0:T(8,128)(2,1)} %get-tuple-element.142, s32[]{:T(128)} %get-tuple-element.130, bf16[2,384,10,64]{1,3,2,0:T(8,128)(2,1)} %get-tuple-element.141), kind=kOutput, calls=%fused_computation.96.clone.1 | convolution fusion | flops 467344288 | bytes 15981466 | tf_op jit(solution)/shard_map/while/body/eval_jaxpr/sub | solution.py:492
  132.0 7.2 %fusion.99 = bf16[2,384,10,64]{1,3,2,0:T(8,128)(2,1)} fusion(bf16[2,384,10,64]{1,3,2,0:T(8,128)(2,1)} %get-tuple-element.131, s32[]{:T(128)} %get-tuple-element.130, f32[10,384,922]{1,2,0:T(8,128)} %get-tuple-element.121, f32[10,384]{1,0:T(8,128)S(1)} %get-tuple-element.122, bf16[2,922,10,64]{1,3,2,0:T(8,128)(2,1)S(1)} %copy-done.10), kind=kOutput, calls=%fused_computation.17.clone.1 | convolution fusion | flops 460508160 | bytes 16081920 | tf_op jit(solution)/shard_map/while/body/eval_jaxpr/hqk,khe->qhe/dot_general | solution.py:495
  139.2 9.5 %fusion.98 = (f32[10,384]{1,0:T(8,128)S(1)}, f32[10,384,922]{1,2,0:T(8,128)}) fusion(pred[922]{0:T(1024)(128)(4,1)S(1)} %get-tuple-element.140, bf16[2,922,10,64]{1,3,2,0:T(8,128)(2,1)} %get-tuple-element.142, s32[]{:T(128)} %get-tuple-element.130, bf16[2,384,10,64]{1,3,2,0:T(8,128)(2,1)} %get-tuple-element.141), kind=kOutput, calls=%fused_computation.96.clone.1 | convolution fusion | flops 467344288 | bytes 15981466 | tf_op jit(solution)/shard_map/while/body/eval_jaxpr/sub | solution.py:492
  148.7 7.2 %fusion.99 = bf16[2,384,10,64]{1,3,2,0:T(8,128)(2,1)} fusion(bf16[2,384,10,64]{1,3,2,0:T(8,128)(2,1)} %get-tuple-element.131, s32[]{:T(128)} %get-tuple-element.130, f32[10,384,922]{1,2,0:T(8,128)} %get-tuple-element.121, f32[10,384]{1,0:T(8,128)S(1)} %get-tuple-element.122, bf16[2,922,10,64]{1,3,2,0:T(8,128)(2,1)S(1)} %copy-done.10), kind=kOutput, calls=%fused_computation.17.clone.1 | convolution fusion | flops 460508160 | bytes 16081920 | tf_op jit(solution)/shard_map/while/body/eval_jaxpr/hqk,khe->qhe/dot_general | solution.py:495
  156.0 3.7 %reshape.90 = bf16[2,2,192,640]{2,1,3,0:T(2,128)(2,1)S(1)} reshape(bf16[2,384,10,64]{1,3,2,0:T(8,128)(2,1)} %get-tuple-element.43) | data formatting | bytes 1966080 | tf_op jit(solution)/shard_map/reshape | solution.py:502
  160.8 1.9 %copy-done = bf16[640,2432]{1,0:T(8,128)(2,1)S(1)} copy-done((bf16[640,2432]{1,0:T(8,128)(2,1)S(1)}, bf16[640,2432]{1,0:T(8,128)(2,1)}, u32[]{:S(2)}) %copy-start) | copy-done | bytes 3112984
  162.7 21.3 %home.1 = f32[96,128]{1,0:T(8,128)S(1)} custom-call(bf16[2,2,192,640]{3,2,1,0:T(8,128)(2,1)S(1)} %copy.24.att_ref, bf16[640,2432]{1,0:T(8,128)(2,1)S(1)} %copy-done, bf16[2,192,64]{2,1,0:T(8,128)(2,1)S(1)} %bitcast.153, bf16[64,2432]{1,0:T(8,128)(2,1)S(1)} %copy-done.1, bf16[64,2432]{1,0:T(8,128)(2,1)S(1)} %bitcast.154, f32[5,2,2432]{2,1,0:T(2,128)S(1)} %bitcast.151, ...), custom_call_target="tpu_custom_call" | custom-call | tf_op jit(solution)/shard_map/home/pallas_call | solution.py:410
  (52 shorter events, 9.4 us)
Async XLA Ops:
  28.4 4.6 %copy-start.11 = (f32[2,2,2432]{2,1,0:T(2,128)S(1)}, f32[2,2,2432]{2,1,0:T(2,128)}, u32[]{:S(2)}) copy-start(f32[2,2,2432]{2,1,0:T(2,128)} %get-tuple-element.42) | copy-start | bytes 116740
  52.1 5.8 %copy-start.12 = (f32[3,64]{1,0:T(4,128)S(1)}, f32[3,64]{1,0:T(4,128)}, u32[]{:S(2)}) copy-start(f32[3,64]{1,0:T(4,128)} %param.25) | copy-start | bytes 2308
  111.2 1.2 copy-start.8
  111.2 1.5 copy-start.9
  112.7 4.8 %copy-start.13 = (s32[128]{0:T(128)S(1)}, s32[128]{0:T(128)}, u32[]{:S(2)}) copy-start(s32[128]{0:T(128)} %param.17) | copy-start | bytes 1540
  112.7 7.1 %copy-start.7 = (s32[128]{0:T(128)S(1)}, s32[128]{0:T(128)}, u32[]{:S(2)}) copy-start(s32[128]{0:T(128)} %live_ref.1) | copy-start | bytes 1540
  122.4 9.5 %copy-start.10 = (bf16[2,922,10,64]{1,3,2,0:T(8,128)(2,1)S(1)}, bf16[2,922,10,64]{1,3,2,0:T(8,128)(2,1)}, u32[]{:S(2)}) copy-start(bf16[2,922,10,64]{1,3,2,0:T(8,128)(2,1)} %get-tuple-element.139) | copy-start | bytes 7080964 | tf_op jit(solution)/shard_map/while
  139.2 9.5 %copy-start.10 = (bf16[2,922,10,64]{1,3,2,0:T(8,128)(2,1)S(1)}, bf16[2,922,10,64]{1,3,2,0:T(8,128)(2,1)}, u32[]{:S(2)}) copy-start(bf16[2,922,10,64]{1,3,2,0:T(8,128)(2,1)} %get-tuple-element.139) | copy-start | bytes 7080964 | tf_op jit(solution)/shard_map/while
  156.0 4.7 %copy-start.1 = (bf16[64,2432]{1,0:T(8,128)(2,1)S(1)}, bf16[64,2432]{1,0:T(8,128)(2,1)}, u32[]{:S(2)}) copy-start(bf16[64,2432]{1,0:T(8,128)(2,1)} %wemb_ref.1) | copy-start | bytes 933892
  156.0 4.7 %copy-start.2 = (s32[128,96]{1,0:T(8,128)S(1)}, s32[128,96]{1,0:T(8,128)}, u32[]{:S(2)}) copy-start(s32[128,96]{1,0:T(8,128)} %reshape.87.slot_ref) | copy-start | bytes 147460
  156.0 4.8 %copy-start.3 = (f32[1,2,5,2432]{3,1,2,0:T(2,128)S(1)}, f32[1,2,5,2432]{3,1,2,0:T(2,128)}, u32[]{:S(2)}) copy-start(f32[1,2,5,2432]{3,1,2,0:T(2,128)} %param.19) | copy-start | bytes 291844
  156.0 4.8 %copy-start.4 = (bf16[4,96,64]{2,1,0:T(8,128)(2,1)S(1)}, bf16[4,96,64]{2,1,0:T(8,128)(2,1)}, u32[]{:S(2)}) copy-start(bf16[4,96,64]{2,1,0:T(8,128)(2,1)} %get-tuple-element.40) | copy-start | bytes 147460
  156.0 4.8 %copy-start.5 = (bf16[2432,64]{0,1:T(8,128)(2,1)S(1)}, bf16[2432,64]{0,1:T(8,128)(2,1)}, u32[]{:S(2)}) copy-start(bf16[2432,64]{0,1:T(8,128)(2,1)} %param.24) | copy-start | bytes 933892
  156.0 4.8 %copy-start.6 = (f32[96,128]{1,0:T(8,128)S(1)}, f32[96,128]{1,0:T(8,128)}, u32[]{:S(2)}) copy-start(f32[96,128]{1,0:T(8,128)} %lat_ref.3) | copy-start | bytes 147460
  160.8 1.9 %copy-start = (bf16[640,2432]{1,0:T(8,128)(2,1)S(1)}, bf16[640,2432]{1,0:T(8,128)(2,1)}, u32[]{:S(2)}) copy-start(bf16[640,2432]{1,0:T(8,128)(2,1)} %wout_ref.1) | copy-start | bytes 9338884

commit v2 on v1

--- a/solution.py
+++ b/solution.py
@@ -16,6 +16,10 @@
 Z = 8
 XY = 16
 HALF = ROWS // 2
+TEXT_PAD = 160
+KEYS = 2 * ROWS + TEXT_PAD
+WIDTH = 640
+SLABS = WIDTH // 128
 
 GUIDE = 3.5
 STEP = -0.25
@@ -77,9 +81,19 @@
     return jnp.where((matched > 0.5) & (rank == rank_wanted), place + 1.0, 0.0)
 
 
+def head_norm(slab, gains):
+    square = slab * slab
+    lower = iota(slab.shape, 1) < HEAD
+    first = jnp.sum(jnp.where(lower, square, 0.0), axis=-1, keepdims=True) * (1.0 / HEAD)
+    second = jnp.sum(jnp.where(lower, 0.0, square), axis=-1, keepdims=True) * (1.0 / HEAD)
+    return slab * jnp.where(lower, lax.rsqrt(first + EPS), lax.rsqrt(second + EPS)) * gains
+
+
 def deal_kernel(
-    lat_ref, slot_ref, mod_ref, own_ref, par_ref, modp_ref,
-    buf_s, buf_a, buf_b, buf_c, mod_s, ssem_a, rsem_a, ssem_b, rsem_b, msem,
+    lat_ref, slot_ref, mod_ref, gain_ref, text_hbm, wtext_hbm,
+    tok_ref, modp_ref, tk_ref, tv_ref,
+    buf_s, buf_a, buf_b, buf_c, mod_s, text_pairs, text, w_pairs, w_split,
+    ssem_a, rsem_a, ssem_b, rsem_b, msem, tsem,
 ):
     group, core, z, xy = where_am_i()
     me = xy * 2 + core
@@ -105,6 +119,11 @@
     def _(k):
         pl.semaphore_signal(barrier, inc=1, device_id=plane_id(k), device_id_type=MESH)
 
+    text_copy = pltpu.make_async_copy(text_hbm, text_pairs.at[pl.ds(0, TEXT)], tsem.at[0])
+    w_copy = pltpu.make_async_copy(wtext_hbm, w_pairs, tsem.at[1])
+    w_copy.start()
+    text_copy.start()
+    text_pairs[TEXT:] = jnp.zeros((TEXT_PAD - TEXT, 2, D), BF16)
     sender = onehot(iota((256, TILES), 0).astype(F32) == my_buckets_row(slot_ref, group))
     buf_s[...] = (
         jnp.dot(sender, lat_ref[...].astype(BF16), preferred_element_type=F32)
@@ -138,6 +157,17 @@
     )
     mod_copy.start()
     buf_a[z] = buf_s[z]
+
+    part_row = iota((256, 256), 0)
+    part = onehot(iota((256, 256), 1) == (part_row & 127) * 2 + (part_row >> 7))
+    w_copy.wait()
+
+    @pl.loop(0, D // 128)
+    def _(i):
+        rows = pl.ds(pl.multiple_of(i * 128, 128), 128)
+        both = jnp.dot(part, w_pairs[rows].reshape(256, WIDTH), preferred_element_type=F32)
+        w_split[0, rows, :] = both[:128].astype(BF16)
+        w_split[1, rows, :] = both[128:].astype(BF16)
 
     row = iota((512, 1), 0)
     low = group - lax.rem(group, 2)
@@ -190,16 +220,38 @@
 
     buf_c[core, xy] = buf_b[lax.div(xy, 2)]
 
+    text_copy.wait()
+    text[...] = text_pairs[...].reshape(2 * TEXT_PAD, D)
+    text_row = iota((2 * TEXT_PAD, 2 * TEXT_PAD), 0)
+    branch = jnp.where(text_row >= TEXT_PAD, 1, 0)
+    part_text = onehot(
+        iota((2 * TEXT_PAD, 2 * TEXT_PAD), 1) == (text_row - branch * TEXT_PAD) * 2 + branch
+    )
+    for c, out in ((0, tk_ref), (1, tv_ref)):
+        projected = jnp.dot(text[...], w_split[c], preferred_element_type=F32)
+        if c == 0:
+            projected = jnp.concatenate(
+                [
+                    head_norm(projected[:, i * 128:(i + 1) * 128], gain_ref[2:3, :])
+                    for i in range(SLABS)
+                ],
+                axis=1,
+            )
+        out[...] = (
+            jnp.dot(part_text, projected.astype(BF16), preferred_element_type=F32)
+            .astype(BF16).reshape(2, TEXT_PAD, WIDTH)
+        )
+
     @pl.loop(1, 2 * XY)
     def _(k):
         come_b(k).wait_recv()
 
     for half in range(2):
         landed = buf_c[half].reshape(512, 128)
-        for take, out in ((take_own, own_ref), (take_par, par_ref)):
+        for side, take in ((0, take_own), (1, take_par)):
             tiles = jnp.dot(take, landed, preferred_element_type=F32).astype(BF16)
-            out[2 * half] = tiles[:, :CH]
-            out[2 * half + 1] = tiles[:, CH:]
+            tok_ref[side, 2 * half] = tiles[:, :CH]
+            tok_ref[side, 2 * half + 1] = tiles[:, CH:]
 
     mod_copy.wait_recv()
     modp_ref[...] = mod_s[...]
@@ -215,31 +267,40 @@
     mod_copy.wait_send()
 
 
-def deal(latents, slots, mod):
+def deal(latents, slots, mod, gains, text, w_text):
+    anywhere = pl.BlockSpec(memory_space=pltpu.HBM)
     return pl.pallas_call(
         deal_kernel,
         out_shape=(
-            jax.ShapeDtypeStruct((TILE, TILES, CH), BF16),
-            jax.ShapeDtypeStruct((TILE, TILES, CH), BF16),
+            jax.ShapeDtypeStruct((2, TILE, TILES, CH), BF16),
             jax.ShapeDtypeStruct((2, 2, D), F32),
+            jax.ShapeDtypeStruct((2, TEXT_PAD, WIDTH), BF16),
+            jax.ShapeDtypeStruct((2, TEXT_PAD, WIDTH), BF16),
         ),
-        in_specs=[VMEM] * 3,
-        out_specs=(VMEM,) * 3,
+        in_specs=[VMEM] * 4 + [anywhere] * 2,
+        out_specs=(VMEM,) * 4,
         scratch_shapes=[
             pltpu.VMEM((Z, 32, 128), BF16),
             pltpu.VMEM((Z, 32, 128), BF16),
             pltpu.VMEM((Z, 32, 128), BF16),
             pltpu.VMEM((2, XY, 32, 128), BF16),
             pltpu.VMEM((2, 2, D), F32),
+            pltpu.VMEM((TEXT_PAD, 2, D), BF16),
+            pltpu.VMEM((2 * TEXT_PAD, D), BF16),
+            pltpu.VMEM((D, 2, WIDTH), BF16),
+            pltpu.VMEM((2, D, WIDTH), BF16),
             pltpu.SemaphoreType.DMA((Z,)),
             pltpu.SemaphoreType.DMA((Z,)),
             pltpu.SemaphoreType.DMA((2 * XY,)),
             pltpu.SemaphoreType.DMA((2 * XY,)),
             pltpu.SemaphoreType.DMA((2,)),
+            pltpu.SemaphoreType.DMA((2,)),
         ],
-        compiler_params=pltpu.CompilerParams(collective_id=0, has_side_effects=True),
+        compiler_params=pltpu.CompilerParams(
+            collective_id=0, has_side_effects=True, vmem_limit_bytes=40 << 20
+        ),
         name="deal",
-    )(latents, slots, mod)
+    )(latents, slots, mod, gains, text, w_text)
 
 
 CHUNKS = ((0, 512), (512, 512), (1024, 512), (1536, 512), (2048, 384))
@@ -436,70 +497,143 @@
     )(attended, w_out, tokens, w_embed, w_final, mod, live, latents, slots)
 
 
-def layer_norm(inputs):
-    centre = jnp.mean(inputs, axis=-1, keepdims=True)
-    centred = inputs - centre
-    spread = jnp.mean(centred * centred, axis=-1, keepdims=True)
-    return centred * lax.rsqrt(spread + EPS)
-
-
-def head_norm(inputs, gains):
-    square = jnp.mean(inputs * inputs, axis=-1, keepdims=True)
-    return (inputs * lax.rsqrt(square + EPS) * gains).astype(BF16)
+def token_position(shape):
+    row = iota(shape, 0)
+    quarter = sum(jnp.where(row >= TILES * j, 1, 0) for j in range(1, TILE))
+    return (row - quarter * TILES) * TILE + quarter
+
+
+def attend_kernel(
+    tok_ref, wemb_ref, mod_ref, modp_ref, w_hbm, tk_ref, tv_ref, gain_ref, live_ref, partner_ref,
+    out_ref, wbuf, normed, qbuf, kbuf, vbuf, wsem,
+):
+    group = lax.axis_index("groups")
+    mate = partner_ref[group]
+    own_len = live_ref[group]
+    mate_len = jnp.where(mate != group, live_ref[mate], 0)
+
+    def fetch(c):
+        return pltpu.make_async_copy(w_hbm.at[c], wbuf.at[c], wsem.at[c])
+
+    for c in (1, 2, 0):
+        fetch(c).start()
+
+    block = 96
+    for side, source in ((0, mod_ref), (1, modp_ref)):
+        @pl.loop(0, ROWS // block)
+        def _(i):
+            rows = pl.ds(pl.multiple_of(i * block, block), block)
+            hidden = jnp.dot(tok_ref[side, rows, :], wemb_ref[...], preferred_element_type=F32)
+            centred = hidden - jnp.mean(hidden, axis=-1, keepdims=True)
+            spread = jnp.mean(centred * centred, axis=-1, keepdims=True)
+            scaled = centred * lax.rsqrt(spread + EPS)
+            for b in range(2):
+                normed[2 * side + b, rows, :] = (
+                    scaled * (1.0 + source[1, b:b + 1, :]) + source[0, b:b + 1, :]
+                ).astype(BF16)
+
+    slot = token_position((ROWS, 128))
+    text_pad = iota((TEXT_PAD, 128), 0) < TEXT
+    for b in range(2):
+        for s in range(SLABS):
+            lanes = slice(s * 128, (s + 1) * 128)
+            first = jnp.broadcast_to(tk_ref[b, 0:1, lanes], (TEXT_PAD, 128))
+            kbuf[b, s, 2 * ROWS:, :] = jnp.where(text_pad, tk_ref[b, :, lanes], first)
+            vbuf[b, s, 2 * ROWS:, :128] = tv_ref[b, :, lanes]
+            vbuf[b, s, 2 * ROWS:, 128:] = onehot(text_pad)
+
+    fetch(1).wait()
+
+    @pl.loop(0, 4)
+    def _(n):
+        side, b = lax.div(n, 2), lax.rem(n, 2)
+        usable = slot < jnp.where(side == 0, own_len, mate_len)
+        rows = pl.ds(pl.multiple_of(side * ROWS, ROWS), ROWS)
+        keys = jnp.dot(normed[n], wbuf[1], preferred_element_type=F32)
+        for s in range(SLABS):
+            lanes = slice(s * 128, (s + 1) * 128)
+            key = head_norm(keys[:, lanes], gain_ref[1:2, :]).astype(BF16)
+            first = jnp.broadcast_to(tk_ref[b, 0:1, lanes], (ROWS, 128))
+            kbuf[b, s, rows, :] = jnp.where(usable, key, first)
+
+    fetch(2).wait()
+
+    @pl.loop(0, 4)
+    def _(n):
+        side, b = lax.div(n, 2), lax.rem(n, 2)
+        usable = slot < jnp.where(side == 0, own_len, mate_len)
+        rows = pl.ds(pl.multiple_of(side * ROWS, ROWS), ROWS)
+        values = jnp.dot(normed[n], wbuf[2], preferred_element_type=F32)
+        for s in range(SLABS):
+            value = values[:, s * 128:(s + 1) * 128]
+            vbuf[b, s, rows, :128] = jnp.where(usable, value, 0.0).astype(BF16)
+            vbuf[b, s, rows, 128:] = onehot(usable)
+
+    fetch(0).wait()
+
+    @pl.loop(0, 2)
+    def _(b):
+        query = jnp.dot(normed[b], wbuf[0], preferred_element_type=F32)
+        for s in range(SLABS):
+            qbuf[b, s] = head_norm(query[:, s * 128:(s + 1) * 128], gain_ref[0:1, :]).astype(BF16)
+
+    lower = iota((ROWS, 128), 1) < HEAD
+
+    @pl.loop(0, 2 * SLABS)
+    def _(n):
+        b, s = lax.div(n, SLABS), lax.rem(n, SLABS)
+        query, key, value = qbuf[b, s], kbuf[b, s], vbuf[b, s]
+        parts = []
+        for mine in (lower, ~lower):
+            scores = lax.dot_general(
+                jnp.where(mine, query, jnp.zeros_like(query)), key, (((1,), (1,)), ((), ())),
+                preferred_element_type=F32,
+            )
+            highest = jnp.max(scores, axis=-1, keepdims=True)
+            raised = jnp.exp((scores - highest) * HEAD ** (-0.5)).astype(BF16)
+            both = jnp.dot(raised, value, preferred_element_type=F32)
+            parts.append(both[:, :128] / both[:, 128:])
+        out_ref[b, :, pl.ds(pl.multiple_of(s * 128, 128), 128)] = (
+            jnp.where(lower, parts[0], parts[1]).astype(BF16)
+        )
+
+
+def attend(tokens, w_embed, mod, mod_mate, w_qkv, text_key, text_value, gains, live, partner):
+    return pl.pallas_call(
+        attend_kernel,
+        out_shape=jax.ShapeDtypeStruct((2, ROWS, WIDTH), BF16),
+        in_specs=[VMEM] * 4 + [pl.BlockSpec(memory_space=pltpu.HBM)] + [VMEM] * 3 + [SMEM] * 2,
+        out_specs=VMEM,
+        scratch_shapes=[
+            pltpu.VMEM((3, D, WIDTH), BF16),
+            pltpu.VMEM((4, ROWS, D), BF16),
+            pltpu.VMEM((2, SLABS, ROWS, 128), BF16),
+            pltpu.VMEM((2, SLABS, KEYS, 128), BF16),
+            pltpu.VMEM((2, SLABS, KEYS, 256), BF16),
+            pltpu.SemaphoreType.DMA((3,)),
+        ],
+        compiler_params=pltpu.CompilerParams(vmem_limit_bytes=48 << 20),
+        name="attend",
+    )(tokens, w_embed, mod, mod_mate, w_qkv, text_key, text_value, gains, live, partner)
 
 
 def shards(
     latents, tile_slot, live, partner, text_states, modulation,
     w_embed, w_qkv, w_text_kv, w_out, w_final, norm_gains,
 ):
-    group = lax.axis_index("groups")
     slots = tile_slot.reshape(Z * XY, TILES)
     mod = modulation[0].transpose(1, 0, 2)
-    own, par, mod_par = deal(latents, slots, mod)
-    tokens = jnp.concatenate([own.reshape(ROWS, CH), par.reshape(ROWS, CH)], axis=0)
-    hidden = jnp.dot(tokens, w_embed, preferred_element_type=F32)
-    scaled = layer_norm(hidden).reshape(2, 1, ROWS, D)
-    mods = jnp.stack([mod[:2], mod_par])
-    normed = (scaled * (1.0 + mods[:, 1, :, None, :]) + mods[:, 0, :, None, :]).astype(BF16)
-    w3 = w_qkv.transpose(1, 0, 2)
-    local_heads = w_qkv.shape[2] // HEAD
-    query = jnp.dot(normed[0].reshape(2 * ROWS, D), w3[0], preferred_element_type=F32)
-    keys = jnp.dot(normed.reshape(4 * ROWS, D), w3[1], preferred_element_type=F32)
-    values = jnp.dot(normed.reshape(4 * ROWS, D), w3[2], preferred_element_type=F32)
-    query = head_norm(query.reshape(2, ROWS, local_heads, HEAD), norm_gains[0])
-    keys = head_norm(keys.reshape(2, 2, ROWS, local_heads, HEAD), norm_gains[1])
-    values = values.reshape(2, 2, ROWS, local_heads, HEAD).astype(BF16)
-    text_proj = jnp.einsum("btd,dcn->btcn", text_states[0], w_text_kv, preferred_element_type=F32)
-    text_proj = text_proj.reshape(2, TEXT, 2, local_heads, HEAD)
-    text_key = head_norm(text_proj[:, :, 0], norm_gains[2])
-    text_value = text_proj[:, :, 1].astype(BF16)
-    mate = partner[group]
-    own_len = live[group]
-    mate_len = jnp.where(mate != group, live[mate], 0)
-    order = jnp.arange(ROWS, dtype=jnp.int32)
-    position = (order % TILES) * TILE + order // TILES
-    all_keys = jnp.concatenate([text_key, keys[0], keys[1]], axis=1)
-    all_values = jnp.concatenate([text_value, values[0], values[1]], axis=1)
-    usable = jnp.concatenate([jnp.ones((TEXT,), bool), position < own_len, position < mate_len])
-
-    def branch_attention(items):
-        branch_query, branch_keys, branch_values = items
-        scores = jnp.einsum(
-            "qhe,khe->hqk", branch_query, branch_keys, preferred_element_type=F32
-        ) * HEAD ** (-0.5)
-        scores = jnp.where(usable[None, None, :], scores, -1e30)
-        highest = jnp.max(scores, axis=-1, keepdims=True)
-        raised = jnp.exp(scores - highest)
-        summed = jnp.sum(raised, axis=-1, keepdims=True)
-        weights = (raised / summed).astype(BF16)
-        result_heads = jnp.einsum(
-            "hqk,khe->qhe", weights, branch_values, preferred_element_type=F32
-        )
-        return result_heads.astype(BF16)
-
-    attended = lax.map(branch_attention, (query, all_keys, all_values))
+    gains = jnp.concatenate([norm_gains, norm_gains], axis=1)
+    tokens, mod_mate, text_key, text_value = deal(
+        latents, slots, mod, gains, text_states[0].transpose(1, 0, 2), w_text_kv
+    )
+    tokens = tokens.reshape(2, ROWS, CH)
+    attended = attend(
+        tokens, w_embed, mod, mod_mate, w_qkv.transpose(1, 0, 2), text_key, text_value,
+        gains, live, partner,
+    )
     return home(
-        attended.reshape(2, 2, HALF, local_heads * HEAD), w_out, own.reshape(2, HALF, CH),
+        attended.reshape(2, 2, HALF, WIDTH), w_out, tokens[0].reshape(2, HALF, CH),
         w_embed, w_final.T, mod, live, latents, slots,
     )
 

time: 186 us -> 93.3 us (0.50)
  matrix products: 64.8 us -> 0 us
  local copies, waits for them, and re-layouts: 50.7 us -> 7.41 us
  Pallas kernels: 45 us -> 84.3 us
  other arithmetic: 20.9 us -> 0.83 us
  between operations: 3.17 us -> 0.13 us
    dot_general x7 -> x0, matrix products: 45.7 us -> none  [the longest x2 14.5 us: branch_attention(): jnp.einsum('hqk,khe->qhe', weights, branch_values, preferred_element_type...]
    pallas_call x1 -> x2, Pallas kernels: 23.7 us -> 64.1 us  [the longest x1 39.8 us: attend(): pl.pallas_call(attend_kernel, out_shape=jax.ShapeDtypeStruct((2, ROWS, WI...]
    dot_general x4 -> x0, local copies, waits for them, and re-layouts: 20.5 us -> none  [the longest x2 11.4 us: shards(): jnp.dot(normed.reshape(4 * ROWS, D), w3[1], preferred_element_type=F32)]
    sub x2 -> x0, matrix products: 19.1 us -> none  [branch_attention(): raised = jnp.exp(scores - highest)]
    unnamed x28 -> x23, local copies, waits for them, and re-layouts: 20.1 us -> 6.49 us
    convert_element_type x4 -> x0, other arithmetic: 10.5 us -> none  [the longest x1 7.74 us: shards(): (scaled * (1.0 + mods[:, 1, :, None, :]) + mods[:, 0, :, None, :]).astype...]
    reshape x2 -> x0, local copies, waits for them, and re-layouts: 4.69 us -> none  [shards(): attended.reshape(2, 2, HALF, local_heads * HEAD)]
    concatenate x2 -> x1, other arithmetic: 4.85 us -> 0.83 us  [shards(): gains = jnp.concatenate([norm_gains, norm_gains], axis=1)]
where the time goes in v2:
time: 93.3 us; the launch traced here: 92.7 us
  Pallas kernels  84.3 us (90%)
  local copies, waits for them, and re-layouts  7.41 us (8%)
    pallas_call x1, Pallas kernels, attend(): pl.pallas_call(attend_kernel, out_shape=jax.ShapeDtypeStruct((2, ROWS, WI...  39.8 us
    pallas_call x1, Pallas kernels, deal(): pl.pallas_call(deal_kernel, out_shape=(jax.ShapeDtypeStruct((2, TILE, TIL...  24.3 us
    pallas_call x1, Pallas kernels, home(): pl.pallas_call(home_kernel, out_shape=jax.ShapeDtypeStruct((TILES, 128),...  20.3 us
    unnamed x23, local copies, waits for them, and re-layouts  6.49 us

profile of v2, /device:TPU:1, one launch (start us, length us, event | category | flops | bytes accessed | tf_op | source)
XLA Modules:
  0.0 92.7 jit_solution(1722886302239638003)
XLA Ops:
  0.0 0.0 copy-start.5
  0.0 0.0 copy-start.9
  0.0 0.0 copy-start.10
  0.0 0.9 reshape.11.slot_ref
  0.9 0.8 pad_maximum_fusion.gain_ref
  1.8 0.0 copy-start
  1.8 2.8 %copy-done = bf16[2432,2,640]{2,1,0:T(2,128)(2,1)S(1)} copy-done((bf16[2432,2,640]{2,1,0:T(2,128)(2,1)S(1)}, bf16[2432,2,640]{2,1,0:T(2,128)(2,1)}, u32[]{:S(2)}) %copy-start) | copy-done | bytes 6225944
  4.5 1.4 %copy-done.2 = bf16[1,2,154,2432]{3,1,2,0:T(2,128)(2,1)S(1)} copy-done((bf16[1,2,154,2432]{3,1,2,0:T(2,128)(2,1)S(1)}, bf16[1,2,154,2432]{3,1,2,0:T(2,128)(2,1)}, u32[]{:S(2)}) %copy-start.2) | copy-done | bytes 1498136
  5.9 0.9 copy-done.4
  6.8 0.8 copy-done.7
  7.6 24.3 %deal.1 = (bf16[2,4,96,64]{3,2,1,0:T(8,128)(2,1)S(1)}, f32[2,2,2432]{2,1,0:T(2,128)S(1)}, bf16[2,160,640]{2,1,0:T(8,128)(2,1)S(1)}, bf16[2,160,640]{2,1,0:T(8,128)(2,1)S(1)}) custom-call(f32[96,128]{1,0:T(8,128)S(1)} %copy-done.7, s32[128,96]{1,0:T(8,128)S(1)} %reshape.11.slot_ref, f32[5,2,2432]{2,1,0:T(2,128)S(1)} %bitcast.13, ...), custom_call_target="tpu_custom_call" | custom-call | tf_op jit(solution)/shard_map/deal/pallas_call | solution.py:272
  31.9 0.0 copy-start.1
  31.9 0.0 copy-start.6
  31.9 0.0 copy-start.8
  31.9 0.0 copy-done.5
  31.9 0.0 copy-done.9
  32.0 0.0 copy-done.10
  32.0 0.0 copy-done.3
  32.0 39.8 %attend.1 = bf16[2,384,640]{2,1,0:T(8,128)(2,1)S(1)} custom-call(bf16[2,384,64]{2,1,0:T(8,128)(2,1)S(1)} %bitcast.16, bf16[64,2432]{1,0:T(8,128)(2,1)S(1)} %copy-done.3, f32[5,2,2432]{2,1,0:T(2,128)S(1)} %bitcast.14, f32[2,2,2432]{2,1,0:T(2,128)S(1)} %get-tuple-element.10.modp_ref, bf16[3,2432,640]{2,1,0:T(8,128)(2,1)} %bitcast.19, ...), custom_call_target="tpu_custom_call" | custom-call | tf_op jit(solution)/shard_map/attend/pallas_call | solution.py:602
  71.8 0.0 copy-done.1
  71.8 0.0 copy-done.6
  71.8 0.0 copy-done.8
  71.8 20.3 %home.1 = f32[96,128]{1,0:T(8,128)S(1)} custom-call(bf16[2,2,192,640]{3,2,1,0:T(8,128)(2,1)S(1)} %bitcast.11, bf16[640,2432]{1,0:T(8,128)(2,1)S(1)} %copy-done.1, bf16[2,192,64]{2,1,0:T(8,128)(2,1)S(1)} %bitcast.17, bf16[64,2432]{1,0:T(8,128)(2,1)S(1)} %copy-done.3, bf16[64,2432]{1,0:T(8,128)(2,1)S(1)} %bitcast.18, f32[5,2,2432]{2,1,0:T(2,128)S(1)} %bitcast.15, ...), custom_call_target="tpu_custom_call" | custom-call | tf_op jit(solution)/shard_map/home/pallas_call | solution.py:471
  92.1 0.6 copy.14
  (5 shorter events, 0.0 us)
Async XLA Ops:
  0.0 31.9 %copy-start.5 = (f32[1,2,5,2432]{3,1,2,0:T(2,128)S(1)}, f32[1,2,5,2432]{3,1,2,0:T(2,128)}, u32[]{:S(2)}) copy-start(f32[1,2,5,2432]{3,1,2,0:T(2,128)} %param.17) | copy-start | bytes 291844
  0.0 31.9 %copy-start.9 = (s32[128]{0:T(128)S(1)}, s32[128]{0:T(128)}, u32[]{:S(2)}) copy-start(s32[128]{0:T(128)} %live_ref.3) | copy-start | bytes 1540
  0.0 32.0 %copy-start.10 = (s32[128]{0:T(128)S(1)}, s32[128]{0:T(128)}, u32[]{:S(2)}) copy-start(s32[128]{0:T(128)} %partner_ref.1) | copy-start | bytes 1540
  1.8 2.8 %copy-start = (bf16[2432,2,640]{2,1,0:T(2,128)(2,1)S(1)}, bf16[2432,2,640]{2,1,0:T(2,128)(2,1)}, u32[]{:S(2)}) copy-start(bf16[2432,2,640]{2,1,0:T(2,128)(2,1)} %wtext_hbm.1) | copy-start | bytes 18677764
  4.5 1.4 %copy-start.2 = (bf16[1,2,154,2432]{3,1,2,0:T(2,128)(2,1)S(1)}, bf16[1,2,154,2432]{3,1,2,0:T(2,128)(2,1)}, u32[]{:S(2)}) copy-start(bf16[1,2,154,2432]{3,1,2,0:T(2,128)(2,1)} %param.16) | copy-start | bytes 4494340
  5.9 0.9 copy-start.4
  6.8 0.8 copy-start.7
  7.6 24.4 %copy-start.3 = (bf16[64,2432]{1,0:T(8,128)(2,1)S(1)}, bf16[64,2432]{1,0:T(8,128)(2,1)}, u32[]{:S(2)}) copy-start(bf16[64,2432]{1,0:T(8,128)(2,1)} %wemb_ref.3) | copy-start | bytes 933892
  31.9 39.9 %copy-start.1 = (bf16[640,2432]{1,0:T(8,128)(2,1)S(1)}, bf16[640,2432]{1,0:T(8,128)(2,1)}, u32[]{:S(2)}) copy-start(bf16[640,2432]{1,0:T(8,128)(2,1)} %wout_ref.1) | copy-start | bytes 9338884
  31.9 39.9 %copy-start.6 = (bf16[2432,64]{0,1:T(8,128)(2,1)S(1)}, bf16[2432,64]{0,1:T(8,128)(2,1)}, u32[]{:S(2)}) copy-start(bf16[2432,64]{0,1:T(8,128)(2,1)} %param.22) | copy-start | bytes 933892
  31.9 39.9 %copy-start.8 = (f32[96,128]{1,0:T(8,128)S(1)}, f32[96,128]{1,0:T(8,128)}, u32[]{:S(2)}) copy-start(f32[96,128]{1,0:T(8,128)} %lat_ref.3) | copy-start | bytes 147460

commit v3 on v0

v3 whole, which is shorter than its diff:
```python
import functools
import jax
import jax.numpy as jnp
from jax import lax
from jax.experimental import pallas as pl
from jax.experimental.pallas import tpu as pltpu
from jax.sharding import PartitionSpec as P

HEAD = 64
CH = 64
TEXT = 154
TEXT_PAD = 160
ROWS = 384
HALF = ROWS // 2
TILE = 4
TILES = 96
D = 2432
Z = 8
XY = 16
KEYS = 2 * ROWS + TEXT_PAD
WIDTH = 640
SLABS = WIDTH // 128
CHUNKS = ((0, 512), (512, 512), (1024, 512), (1536, 512), (2048, 384))

GUIDE = 3.5
STEP = -0.25
EPS = 1e-06
LOG2E = 1.4426950408889634
F32 = jnp.float32
BF16 = jnp.bfloat16
MESH = pl.DeviceIdType.MESH
NT = (((1,), (1,)), ((), ()))


def iota(shape, axis):
    return lax.broadcasted_iota(jnp.int32, shape, axis)


def onehot(condition):
    return jnp.where(condition, 1.0, 0.0).astype(BF16)


def dot(left, right):
    return jnp.dot(left, right, preferred_element_type=F32)


def group_of(slot):
    return (slot * 43691) >> 22


def head_norm(slab, gains):
    square = slab * slab
    lower = iota(slab.shape, 1) < HEAD
    first = jnp.sum(jnp.where(lower, square, 0.0), axis=-1, keepdims=True) * (1.0 / HEAD)
    second = jnp.sum(jnp.where(lower, 0.0, square), axis=-1, keepdims=True) * (1.0 / HEAD)
    return slab * jnp.where(lower, lax.rsqrt(first + EPS), lax.rsqrt(second + EPS)) * gains


def step_kernel(
    lat_hbm, slot_hbm, mod_hbm, gain_hbm, text_hbm, wtext_hbm, wemb_hbm, wqkv_hbm, wout_hbm,
    wfin_hbm, live_ref, partner_ref, out_ref,
    lat, slot_raw, slot_tab, mod, mod_mate, gain, text_pairs, text, w_pairs, w_split, wemb, wqkv,
    wout, wfin, tk, tv, tok, normed, qbuf, kbuf, vbuf, att, got, hid, vel,
    out_a, in_a, out_b, in_b, home_b, back_b, home_a, back_a,
    lsem, msem, ssem_a, rsem_a, ssem_b, rsem_b, ssem_c, rsem_c, xsend, xrecv,
    hsend_b, hrecv_b, hsend_a, hrecv_a,
):
    group, core = lax.axis_index("groups"), lax.axis_index("mp")
    z, xy = lax.div(group, XY), lax.rem(group, XY)
    other = 1 - core
    mate = group + 1 - 2 * lax.rem(group, 2)
    sibling_id = {"groups": group, "mp": other}
    mate_id = {"groups": mate, "mp": core}
    cross_id = {"groups": mate, "mp": other}

    def z_peer(k):
        return lax.rem(z + k, Z)

    def z_id(k):
        return {"groups": z_peer(k) * XY + xy, "mp": core}

    def plane_peer(k):
        return lax.rem(xy + k, XY)

    def plane_id(k):
        return {"groups": z * XY + plane_peer(k), "mp": core}

    def remote(src, dst, send, recv, to):
        return pltpu.make_async_remote_copy(
            src_ref=src, dst_ref=dst, send_sem=send, recv_sem=recv,
            device_id=to, device_id_type=MESH,
        )

    barrier = pltpu.get_barrier_semaphore()

    @pl.loop(1, Z)
    def _(k):
        pl.semaphore_signal(barrier, inc=1, device_id=z_id(k), device_id_type=MESH)

    @pl.loop(1, XY)
    def _(k):
        pl.semaphore_signal(barrier, inc=1, device_id=plane_id(k), device_id_type=MESH)

    for to in (sibling_id, cross_id):
        pl.semaphore_signal(barrier, inc=1, device_id=to, device_id_type=MESH)

    loads = [
        (slot_hbm, slot_raw), (lat_hbm, lat), (text_hbm, text_pairs.at[pl.ds(0, TEXT)]),
        (wtext_hbm, w_pairs), (gain_hbm, gain), (mod_hbm, mod), (wemb_hbm, wemb),
    ] + [
        (wqkv_hbm.at[c], wqkv.at[:, pl.ds(c * WIDTH, WIDTH)]) for c in range(3)
    ] + [(wout_hbm, wout), (wfin_hbm, wfin)]
    loads = [
        pltpu.make_async_copy(src, dst, lsem.at[i]) for i, (src, dst) in enumerate(loads)
    ]
    (slot_load, lat_load, text_load, wtext_load, gain_load, mod_load, wemb_load,
     q_load, k_load, v_load, wout_load, wfin_load) = loads
    for load in loads:
        load.start()
    text_pairs[TEXT:] = jnp.zeros((TEXT_PAD - TEXT, 2, D), BF16)

    slot_load.wait()
    three = jnp.concatenate([slot_raw[pl.ds(i, 32, stride=3), :] for i in range(3)], axis=1)
    for k in range(4):
        slot_tab[32 * k:32 * (k + 1), :] = three[:, TILES * k:TILES * (k + 1)]

    mine = slot_tab[pl.ds(lax.rem(group, 4) * 32 + lax.div(group, 4), 1), :]
    mine = jnp.broadcast_to(group_of(mine).astype(F32), (TILES, TILES))
    across, down = iota((TILES, TILES), 1), iota((TILES, TILES), 0)
    column = jnp.sum(jnp.where(across == down, mine, 0.0), axis=1, keepdims=True)
    same = mine == column
    bucket_row = 2.0 * mine[:1] + jnp.sum(
        jnp.where(same & (down < across), 1.0, 0.0), axis=0, keepdims=True
    )
    bucket_column = 2.0 * column + jnp.sum(
        jnp.where(same & (across < down), 1.0, 0.0), axis=1, keepdims=True
    )
    sender = onehot(iota((256, TILES), 0).astype(F32) == bucket_row)
    lat_load.wait()
    out_a[...] = dot(sender, lat[...].astype(BF16)).astype(BF16).reshape(Z, 32, 128)

    pl.semaphore_wait(barrier, Z - 1 + XY - 1 + 2)

    def send_a(k):
        return remote(out_a.at[z_peer(k)], in_a.at[z], ssem_a.at[k], rsem_a.at[z], z_id(k))

    def come_a(k):
        at = z_peer(k)
        return remote(out_a.at[at], in_a.at[at], ssem_a.at[k], rsem_a.at[at], z_id(k))

    @pl.loop(1, Z)
    def _(k):
        send_a(k).start()

    mod_copy = remote(mod_hbm.at[pl.ds(0, 2)], mod_mate, msem.at[0], msem.at[1], mate_id)
    mod_copy.start()
    in_a[z] = out_a[z]

    part_row = iota((256, 256), 0)
    part = onehot(iota((256, 256), 1) == (part_row & 127) * 2 + (part_row >> 7))
    wtext_load.wait()

    @pl.loop(0, D // 128)
    def _(i):
        rows = pl.ds(pl.multiple_of(i * 128, 128), 128)
        both = dot(part, w_pairs[rows].reshape(256, WIDTH))
        w_split[0, rows, :] = both[:128].astype(BF16)
        w_split[1, rows, :] = both[128:].astype(BF16)

    @pl.loop(1, Z)
    def _(k):
        come_a(k).wait_recv()

    row, col = iota((256, 256), 0), iota((256, 256), 1)
    reorder = onehot(col == (row & 7) * 32 + (row >> 4) * 2 + ((row >> 3) & 1))
    out_b[...] = dot(reorder, in_a[...].reshape(256, 128)).astype(BF16).reshape(XY, 16, 128)

    def send_b(k):
        return remote(out_b.at[plane_peer(k)], in_b.at[xy], ssem_b.at[k], rsem_b.at[xy], plane_id(k))

    def come_b(k):
        at = plane_peer(k)
        return remote(out_b.at[at], in_b.at[at], ssem_b.at[k], rsem_b.at[at], plane_id(k))

    @pl.loop(1, XY)
    def _(k):
        send_b(k).start()

    in_b[xy] = out_b[xy]

    slot = slot_tab[...]
    target = group_of(slot)
    placed = slot - target * TILES
    row = iota((256, 1), 0)
    pick = onehot(
        iota((256, Z * XY), 1) == ((row >> 4) & 3) * 32 + (row & 7) * 4 + (row >> 6)
    )
    goal = dot(pick, target.astype(F32).astype(BF16))
    place = dot(pick, placed.astype(F32).astype(BF16))
    matched = jnp.where(goal == group.astype(F32), 1.0, 0.0)
    before = onehot(iota((TILES, TILES), 0) < iota((TILES, TILES), 1))
    rank = dot(matched.astype(BF16), before)
    brought = jnp.where(
        (matched > 0.5) & (rank == ((row >> 3) & 1).astype(F32)), place + 1.0, 0.0
    )
    spot_row = lax.dot_general(
        jnp.ones((8, TILES), BF16), brought.astype(BF16), NT, preferred_element_type=F32
    )[:1]
    spot_column = jnp.sum(brought, axis=1, keepdims=True)
    settle = onehot(iota((TILES, 256), 0).astype(F32) + 1.0 == spot_row)

    text_load.wait()
    gain_load.wait()
    text[...] = text_pairs[...].reshape(2 * TEXT_PAD, D)
    text_row, text_col = (iota((2 * TEXT_PAD, 2 * TEXT_PAD), i) for i in range(2))
    branch = jnp.where(text_row >= TEXT_PAD, 1, 0)
    part_text = onehot(text_col == (text_row - branch * TEXT_PAD) * 2 + branch)

    def project_text(c, out):
        projected = dot(text[...], w_split[c])
        if c == 0:
            slabs = [
                head_norm(projected[:, i * 128:(i + 1) * 128], gain[2:3, :]) for i in range(SLABS)
            ]
            projected = jnp.concatenate(slabs, axis=1)
        out[...] = dot(part_text, projected.astype(BF16)).astype(BF16).reshape(2, TEXT_PAD, WIDTH)

    project_text(0, tk)

    @pl.loop(1, XY)
    def _(k):
        come_b(k).wait_recv()

    tok[0, core] = dot(settle, in_b[...].reshape(256, 128)).astype(BF16)

    def send_c(i):
        side, to = ((1, mate_id), (0, sibling_id), (1, cross_id))[i]
        return remote(tok.at[0, core], tok.at[side, core], ssem_c.at[i], rsem_c.at[i], to)

    def come_c(i):
        side, half, to = ((1, core, mate_id), (0, other, sibling_id), (1, other, cross_id))[i]
        return remote(tok.at[0, core], tok.at[side, half], ssem_c.at[i], rsem_c.at[i], to)

    for i in range(3):
        send_c(i).start()

    project_text(1, tv)
    text_used = iota((TEXT_PAD, 128), 0) < TEXT
    for b in range(2):
        for s in range(SLABS):
            lanes = slice(s * 128, (s + 1) * 128)
            first = jnp.broadcast_to(tk[b, 0:1, lanes], (TEXT_PAD, 128))
            kbuf[b, s, 2 * ROWS:, :] = jnp.where(text_used, tk[b, :, lanes], first)
            vbuf[b, s, 2 * ROWS:, :128] = tv[b, :, lanes]
            vbuf[b, s, 2 * ROWS:, 128:] = onehot(text_used)

    own_len = live_ref[group]
    mate_len = jnp.where(partner_ref[group] != group, live_ref[mate], 0)
    row = iota((ROWS, 128), 0)
    quarter = sum(jnp.where(row >= TILES * j, 1, 0) for j in range(1, TILE))
    position = (row - quarter * TILES) * TILE + quarter

    for load in (mod_load, wemb_load, q_load, k_load, v_load):
        load.wait()
    for i in range(3):
        come_c(i).wait_recv()
    mod_copy.wait_recv()

    def embed(side, half, source):
        for low in range(2):
            piece = tok[side, half][:, low * CH:(low + 1) * CH]
            hidden = dot(piece, wemb[...])
            centred = hidden - jnp.mean(hidden, axis=-1, keepdims=True)
            spread = jnp.mean(centred * centred, axis=-1, keepdims=True)
            scaled = centred * lax.rsqrt(spread + EPS)
            rows = pl.ds(pl.multiple_of((2 * half + low) * TILES, 32), TILES)
            for b in range(2):
                normed[2 * side + b, rows, :] = (
                    scaled * (1.0 + source[1, b:b + 1, :]) + source[0, b:b + 1, :]
                ).astype(BF16)

    def put(side, b, slab_index, slab):
        usable = position < (own_len if side == 0 else mate_len)
        rows = slice(side * ROWS, (side + 1) * ROWS)
        c, s = divmod(slab_index, SLABS)
        if c == 0:
            qbuf[b, s] = head_norm(slab, gain[0:1, :]).astype(BF16)
        elif c == 1:
            key = head_norm(slab, gain[1:2, :]).astype(BF16)
            first = jnp.broadcast_to(tk[b, 0:1, s * 128:(s + 1) * 128], key.shape)
            kbuf[b, s, rows, :] = jnp.where(usable, key, first)
        else:
            vbuf[b, s, rows, :128] = jnp.where(usable, slab, 0.0).astype(BF16)
            vbuf[b, s, rows, 128:] = onehot(usable)

    def project(side, b, slabs):
        for i in range(0, len(slabs), 2):
            pair = slabs[i:i + 2]
            out = dot(normed[2 * side + b], wqkv[:, pair[0] * 128:(pair[-1] + 1) * 128])
            for t, slab_index in enumerate(pair):
                put(side, b, slab_index, out[:, t * 128:(t + 1) * 128])

    @pl.loop(0, 2)
    def _(half):
        embed(0, half, mod)

    @pl.loop(0, 2)
    def _(b):
        project(0, b, list(range(3 * SLABS)))
        embed(1, b, mod_mate)

    @pl.loop(0, 2)
    def _(b):
        project(1, b, list(range(SLABS, 3 * SLABS)))

    def half_rows(b):
        return slice(b * HALF, (b + 1) * HALF) if isinstance(b, int) else pl.ds(
            pl.multiple_of(b * HALF, HALF), HALF
        )

    def exchange(b):
        return remote(
            normed.at[0, half_rows(b)], got.at[b], xsend.at[b], xrecv.at[b], sibling_id
        )

    def project_out(b, half, into):
        rows = att[b, pl.ds(pl.multiple_of(half * HALF, HALF), HALF), :]
        for start, size in CHUNKS:
            normed[into, half_rows(b), start:start + size] = dot(
                rows, wout[:, start:start + size]
            ).astype(BF16)

    lower = iota((ROWS, 128), 1) < HEAD
    wout_load.wait()

    @pl.loop(0, 2)
    def _(b):
        for s in range(SLABS):
            query, key, value = qbuf[b, s], kbuf[b, s], vbuf[b, s]
            parts = []
            for head in (lower, ~lower):
                scores = lax.dot_general(
                    jnp.where(head, query, jnp.zeros_like(query)), key, NT,
                    preferred_element_type=F32,
                )
                highest = jnp.max(scores, axis=-1, keepdims=True)
                raised = jnp.exp2((scores - highest) * (HEAD ** (-0.5) * LOG2E)).astype(BF16)
                both = dot(raised, value)
                parts.append(both[:, :128] / both[:, 128:])
            att[b, :, s * 128:(s + 1) * 128] = jnp.where(lower, parts[0], parts[1]).astype(BF16)
        project_out(b, other, 0)
        exchange(b).start()

    wfin_load.wait()
    for b in range(2):
        project_out(b, core, 1)
    for low in range(2):
        piece = tok[0, core][:, low * CH:(low + 1) * CH]
        for start, size in CHUNKS:
            hid[low * TILES:(low + 1) * TILES, start:start + size] = dot(
                piece, wemb[:, start:start + size]
            )

    block = 48
    for b in range(2):
        exchange(b).wait_recv()
        gate, shift, scale = (mod[i, b:b + 1, :] for i in (2, 3, 4))

        @pl.loop(0, HALF // block)
        def _(i):
            rows = pl.ds(pl.multiple_of(i * block, block), block)
            kept = normed[1, pl.ds(pl.multiple_of(b * HALF + i * block, block), block), :]
            mixed = kept.astype(F32) + got[b, rows, :].astype(F32)
            state = hid[rows, :] + gate * mixed
            centred = state - jnp.mean(state, axis=-1, keepdims=True)
            spread = jnp.mean(centred * centred, axis=-1, keepdims=True)
            final = (centred * lax.rsqrt(spread + EPS) * (1.0 + scale) + shift).astype(BF16)
            vel[b, rows, :] = lax.dot_general(final, wfin[...], NT, preferred_element_type=F32)

    guided = vel[1] + GUIDE * (vel[0] - vel[1])
    row = iota((HALF, CH), 0)
    upper = jnp.where(row >= TILES, 1, 0)
    position = (row - upper * TILES) * TILE + 2 * core + upper
    change = jnp.where(position < own_len, STEP * guided, 0.0)
    change = jnp.concatenate([change[:TILES], change[TILES:]], axis=1).astype(BF16)
    unsettle = onehot(spot_column == iota((256, TILES), 1).astype(F32) + 1.0)
    home_b[...] = dot(unsettle, change).astype(BF16).reshape(XY, 16, 128)

    def return_b(k):
        return remote(
            home_b.at[plane_peer(k)], back_b.at[xy], hsend_b.at[k], hrecv_b.at[xy], plane_id(k)
        )

    def arrive_b(k):
        at = plane_peer(k)
        return remote(home_b.at[at], back_b.at[at], hsend_b.at[k], hrecv_b.at[at], plane_id(k))

    @pl.loop(1, XY)
    def _(k):
        return_b(k).start()

    back_b[xy] = home_b[xy]
    row, col = iota((256, 256), 0), iota((256, 256), 1)
    reorder = onehot(col == ((row >> 1) & 15) * 16 + (row & 1) * 8 + (row >> 5))
    collect = onehot(iota((TILES, 256), 1).astype(F32) == bucket_column)

    @pl.loop(1, XY)
    def _(k):
        arrive_b(k).wait_recv()

    home_a[...] = dot(reorder, back_b[...].reshape(256, 128)).astype(BF16).reshape(Z, 32, 128)

    def return_a(k):
        return remote(
            home_a.at[z_peer(k)], back_a.at[z], hsend_a.at[k], hrecv_a.at[z], z_id(k)
        )

    def arrive_a(k):
        at = z_peer(k)
        return remote(home_a.at[at], back_a.at[at], hsend_a.at[k], hrecv_a.at[at], z_id(k))

    @pl.loop(1, Z)
    def _(k):
        return_a(k).start()

    back_a[z] = home_a[z]

    @pl.loop(1, Z)
    def _(k):
        send_a(k).wait_send()

    @pl.loop(1, XY)
    def _(k):
        send_b(k).wait_send()
        return_b(k).wait_send()

    for i in range(3):
        send_c(i).wait_send()
    mod_copy.wait_send()
    for b in range(2):
        exchange(b).wait_send()

    @pl.loop(1, Z)
    def _(k):
        arrive_a(k).wait_recv()

    out_ref[...] = lat[...] + dot(collect, back_a[...].reshape(256, 128))

    @pl.loop(1, Z)
    def _(k):
        return_a(k).wait_send()


def step(*operands):
    hbm = pl.BlockSpec(memory_space=pltpu.HBM)
    smem = pl.BlockSpec(memory_space=pltpu.SMEM)
    narrow, wide = pltpu.VMEM((Z, 32, 128), BF16), pltpu.VMEM((XY, 16, 128), BF16)
    dma = pltpu.SemaphoreType.DMA
    return pl.pallas_call(
        step_kernel,
        out_shape=jax.ShapeDtypeStruct((TILES, 128), F32),
        in_specs=[hbm] * 10 + [smem] * 2,
        out_specs=pl.BlockSpec(memory_space=pltpu.VMEM),
        scratch_shapes=[
            pltpu.VMEM((TILES, 128), F32),
            pltpu.VMEM((TILES, 128), jnp.int32),
            pltpu.VMEM((Z * XY, TILES), jnp.int32),
            pltpu.VMEM((5, 2, D), F32),
            pltpu.VMEM((2, 2, D), F32),
            pltpu.VMEM((3, 128), F32),
            pltpu.VMEM((TEXT_PAD, 2, D), BF16),
            pltpu.VMEM((2 * TEXT_PAD, D), BF16),
            pltpu.VMEM((D, 2, WIDTH), BF16),
            pltpu.VMEM((2, D, WIDTH), BF16),
            pltpu.VMEM((CH, D), BF16),
            pltpu.VMEM((D, 3 * WIDTH), BF16),
            pltpu.VMEM((WIDTH, D), BF16),
            pltpu.VMEM((CH, D), BF16),
            pltpu.VMEM((2, TEXT_PAD, WIDTH), BF16),
            pltpu.VMEM((2, TEXT_PAD, WIDTH), BF16),
            pltpu.VMEM((2, 2, TILES, 128), BF16),
            pltpu.VMEM((4, ROWS, D), BF16),
            pltpu.VMEM((2, SLABS, ROWS, 128), BF16),
            pltpu.VMEM((2, SLABS, KEYS, 128), BF16),
            pltpu.VMEM((2, SLABS, KEYS, 256), BF16),
            pltpu.VMEM((2, ROWS, WIDTH), BF16),
            pltpu.VMEM((2, HALF, D), BF16),
            pltpu.VMEM((HALF, D), F32),
            pltpu.VMEM((2, HALF, CH), F32),
            narrow, narrow, wide, wide, wide, wide, narrow, narrow,
            dma((12,)), dma((2,)), dma((Z,)), dma((Z,)), dma((XY,)), dma((XY,)),
            dma((3,)), dma((3,)), dma((2,)), dma((2,)),
            dma((XY,)), dma((XY,)), dma((Z,)), dma((Z,)),
        ],
        compiler_params=pltpu.CompilerParams(
            collective_id=0, has_side_effects=True, vmem_limit_bytes=62 << 20
        ),
        name="step",
    )(*operands)


def shards(
    latents, tile_slot, live, partner, text_states, modulation,
    w_embed, w_qkv, w_text_kv, w_out, w_final, norm_gains,
):
    return step(
        latents, tile_slot.reshape(TILES, 128), modulation[0].transpose(1, 0, 2),
        jnp.concatenate([norm_gains, norm_gains], axis=1), text_states[0].transpose(1, 0, 2),
        w_text_kv, w_embed, w_qkv.transpose(1, 0, 2), w_out, w_final.T, live, partner,
    )


def solution(mesh):
    placed = (
        P("groups", "mp"), P(), P(), P(),
        P("groups", None, None, None), P("groups", None, None, None),
        P(), P(None, None, "mp"), P(None, None, "mp"), P("mp", None), P(), P(),
    )
    return jax.shard_map(
        shards, mesh=mesh, in_specs=placed, out_specs=P("groups", "mp"), check_vma=False
    )
```

time: 243 us -> 76 us (0.31)
  Pallas kernels: 0 us -> 73 us
  matrix products: 63.5 us -> 0 us
  waiting for transfers between devices: 59.7 us -> 0 us
  local copies, waits for them, and re-layouts: 29.9 us -> 1.42 us
  blocking collectives: 26.7 us -> 0 us
  other arithmetic: 27.7 us -> 1.41 us
  starting transfers between devices: 17.7 us -> 0 us
  between operations: 16.7 us -> 0.01 us
    pallas_call x0 -> x1, Pallas kernels: none -> 73 us  [step(): pl.pallas_call(step_kernel, out_shape=jax.ShapeDtypeStruct((TILES, 128),...]
    dot_general x11 -> x0, matrix products: 44.7 us -> none  [the longest x2 15.2 us: branch_attention(): jnp.einsum('hqk,khe->qhe', weights, branch_values, preferred_element_type...]
    psum x1 -> x0, waiting for transfers between devices: 36.1 us -> none  [shards(): mixed = lax.psum(partial_sum.astype(jnp.bfloat16), 'mp').astype(jnp.float32)]
    all_to_all x1 -> x0, blocking collectives: 24.1 us -> none  [shards(): lax.all_to_all(homeward.astype(jnp.bfloat16), 'groups', split_axis=0, con...]
    ppermute x1 -> x0, waiting for transfers between devices: 23.6 us -> none  [partner_2(): return lax.ppermute(value, axis, pairs)]
    unnamed x44 -> x1, local copies, waits for them, and re-layouts: 21.3 us -> 1.42 us
    sub x2 -> x0, matrix products: 18.8 us -> none  [branch_attention(): raised = jnp.exp(scores - highest)]
    all_to_all x1 -> x0, starting transfers between devices: 16.9 us -> none  [shards(): lax.all_to_all(outbound.astype(jnp.bfloat16), 'groups', split_axis=0, con...]
  transfers between devices with their start and end apart: 3 -> 0, of which waited for: 2 -> 0; matrix products, arithmetic and copies ran while one was open for 15% -> 0% of each run, Pallas kernels for 0% -> 0%
where the time goes in v3:
time: 76 us; the launch traced here: 75.8 us
  Pallas kernels  73 us (96%)
  local copies, waits for them, and re-layouts  1.42 us (2%)
  other arithmetic  1.41 us (2%)
    pallas_call x1, Pallas kernels, step(): pl.pallas_call(step_kernel, out_shape=jax.ShapeDtypeStruct((TILES, 128),...  73 us

profile of v3, /device:TPU:1, one launch (start us, length us, event | category | flops | bytes accessed | tf_op | source)
XLA Modules:
  0.0 75.8 jit_solution(2931597214112359634)
XLA Ops:
  0.0 1.4 %pad_maximum_fusion.gain_hbm = f32[3,128]{1,0:T(4,128)} fusion(f32[3,64]{1,0:T(4,128)} %param.23), kind=kLoop, calls=%fused_computation | loop fusion | flops 384 | bytes 2304 | tf_op jit(solution)/shard_map/concatenate | solution.py:508
  1.4 73.0 %step.1 = f32[96,128]{1,0:T(8,128)} custom-call(f32[96,128]{1,0:T(8,128)} %lat_hbm.1, s32[96,128]{1,0:T(8,128)} %bitcast.13, f32[5,2,2432]{2,1,0:T(2,128)} %bitcast.12, f32[3,128]{1,0:T(4,128)} %pad_maximum_fusion.gain_hbm, bf16[154,2,2432]{2,1,0:T(2,128)(2,1)} %bitcast.10, bf16[2432,2,640]{2,1,0:T(2,128)(2,1)} %wtext_hbm.1, bf16[64,2432]{1,0:T(8,128)(2,1)} %wemb_hbm.1, ...), custom_call_target="tpu_custom_call" | custom-call | tf_op jit(solution)/shard_map/step/pallas_call | solution.py:459
  74.4 1.4 %copy.14 = f32[96,128]{1,0:T(8,128)} copy(f32[96,128]{1,0:T(8,128)} %step.1) | data formatting | bytes 98304

commit v4 on v3

--- a/solution.py
+++ b/solution.py
@@ -59,8 +59,8 @@
 def step_kernel(
     lat_hbm, slot_hbm, mod_hbm, gain_hbm, text_hbm, wtext_hbm, wemb_hbm, wqkv_hbm, wout_hbm,
     wfin_hbm, live_ref, partner_ref, out_ref,
-    lat, slot_raw, slot_tab, mod, mod_mate, gain, text_pairs, text, w_pairs, w_split, wemb, wqkv,
-    wout, wfin, tk, tv, tok, normed, qbuf, kbuf, vbuf, att, got, hid, vel,
+    lat, slot_raw, slot_tab, mod, mod_mate, gain_half, gain, text_pairs, text, w_pairs, w_split, wemb, wqkv,
+    wout, wfin, tk, tv, tok, normed, qbuf, kbuf, vbuf, att, got, hid, line, vel, landing,
     out_a, in_a, out_b, in_b, home_b, back_b, home_a, back_a,
     lsem, msem, ssem_a, rsem_a, ssem_b, rsem_b, ssem_c, rsem_c, xsend, xrecv,
     hsend_b, hrecv_b, hsend_a, hrecv_a,
@@ -71,7 +71,6 @@
     mate = group + 1 - 2 * lax.rem(group, 2)
     sibling_id = {"groups": group, "mp": other}
     mate_id = {"groups": mate, "mp": core}
-    cross_id = {"groups": mate, "mp": other}
 
     def z_peer(k):
         return lax.rem(z + k, Z)
@@ -101,12 +100,11 @@
     def _(k):
         pl.semaphore_signal(barrier, inc=1, device_id=plane_id(k), device_id_type=MESH)
 
-    for to in (sibling_id, cross_id):
-        pl.semaphore_signal(barrier, inc=1, device_id=to, device_id_type=MESH)
+    pl.semaphore_signal(barrier, inc=1, device_id=sibling_id, device_id_type=MESH)
 
     loads = [
         (slot_hbm, slot_raw), (lat_hbm, lat), (text_hbm, text_pairs.at[pl.ds(0, TEXT)]),
-        (wtext_hbm, w_pairs), (gain_hbm, gain), (mod_hbm, mod), (wemb_hbm, wemb),
+        (wtext_hbm, w_pairs), (gain_hbm, gain_half), (mod_hbm, mod), (wemb_hbm, wemb),
     ] + [
         (wqkv_hbm.at[c], wqkv.at[:, pl.ds(c * WIDTH, WIDTH)]) for c in range(3)
     ] + [(wout_hbm, wout), (wfin_hbm, wfin)]
@@ -139,7 +137,7 @@
     lat_load.wait()
     out_a[...] = dot(sender, lat[...].astype(BF16)).astype(BF16).reshape(Z, 32, 128)
 
-    pl.semaphore_wait(barrier, Z - 1 + XY - 1 + 2)
+    pl.semaphore_wait(barrier, Z - 1 + XY - 1 + 1)
 
     def send_a(k):
         return remote(out_a.at[z_peer(k)], in_a.at[z], ssem_a.at[k], rsem_a.at[z], z_id(k))
@@ -167,50 +165,60 @@
         w_split[0, rows, :] = both[:128].astype(BF16)
         w_split[1, rows, :] = both[128:].astype(BF16)
 
-    @pl.loop(1, Z)
-    def _(k):
-        come_a(k).wait_recv()
-
     row, col = iota((256, 256), 0), iota((256, 256), 1)
     reorder = onehot(col == (row & 7) * 32 + (row >> 4) * 2 + ((row >> 3) & 1))
-    out_b[...] = dot(reorder, in_a[...].reshape(256, 128)).astype(BF16).reshape(XY, 16, 128)
+
+    @pl.loop(1, Z)
+    def _(k):
+        come_a(k).wait_recv()
+
+    out_b[...] = dot(reorder, in_a[...].reshape(256, 128)).astype(BF16).reshape(XY // 2, 32, 128)
 
     def send_b(k):
-        return remote(out_b.at[plane_peer(k)], in_b.at[xy], ssem_b.at[k], rsem_b.at[xy], plane_id(k))
+        return remote(
+            out_b.at[lax.div(plane_peer(k), 2)], in_b.at[xy], ssem_b.at[k], rsem_b.at[xy],
+            plane_id(k),
+        )
 
     def come_b(k):
         at = plane_peer(k)
-        return remote(out_b.at[at], in_b.at[at], ssem_b.at[k], rsem_b.at[at], plane_id(k))
+        return remote(
+            out_b.at[lax.div(at, 2)], in_b.at[at], ssem_b.at[k], rsem_b.at[at], plane_id(k)
+        )
 
     @pl.loop(1, XY)
     def _(k):
         send_b(k).start()
 
-    in_b[xy] = out_b[xy]
+    in_b[xy] = out_b[lax.div(xy, 2)]
 
     slot = slot_tab[...]
     target = group_of(slot)
     placed = slot - target * TILES
-    row = iota((256, 1), 0)
+    row = iota((512, 1), 0)
+    bit = lax.rem(group, 2)
     pick = onehot(
-        iota((256, Z * XY), 1) == ((row >> 4) & 3) * 32 + (row & 7) * 4 + (row >> 6)
+        iota((512, Z * XY), 1) == ((row >> 5) & 3) * 32 + (row & 7) * 4 + (row >> 7)
     )
     goal = dot(pick, target.astype(F32).astype(BF16))
     place = dot(pick, placed.astype(F32).astype(BF16))
-    matched = jnp.where(goal == group.astype(F32), 1.0, 0.0)
+    matched = jnp.where(goal == (group - bit + ((row >> 4) & 1)).astype(F32), 1.0, 0.0)
     before = onehot(iota((TILES, TILES), 0) < iota((TILES, TILES), 1))
     rank = dot(matched.astype(BF16), before)
     brought = jnp.where(
         (matched > 0.5) & (rank == ((row >> 3) & 1).astype(F32)), place + 1.0, 0.0
     )
+    landing[...] = brought.reshape(XY, 2, 16, TILES)
     spot_row = lax.dot_general(
         jnp.ones((8, TILES), BF16), brought.astype(BF16), NT, preferred_element_type=F32
     )[:1]
-    spot_column = jnp.sum(brought, axis=1, keepdims=True)
-    settle = onehot(iota((TILES, 256), 0).astype(F32) + 1.0 == spot_row)
+    hit = iota((TILES, 512), 0).astype(F32) + 1.0 == spot_row
+    member = (iota((TILES, 512), 1) >> 4) & 1
+    settle = jnp.concatenate([onehot(hit & (member == bit)), onehot(hit & (member != bit))], axis=0)
 
     text_load.wait()
     gain_load.wait()
+    gain[...] = jnp.concatenate([gain_half[...], gain_half[...]], axis=1)
     text[...] = text_pairs[...].reshape(2 * TEXT_PAD, D)
     text_row, text_col = (iota((2 * TEXT_PAD, 2 * TEXT_PAD), i) for i in range(2))
     branch = jnp.where(text_row >= TEXT_PAD, 1, 0)
@@ -231,20 +239,15 @@
     def _(k):
         come_b(k).wait_recv()
 
-    tok[0, core] = dot(settle, in_b[...].reshape(256, 128)).astype(BF16)
-
-    def send_c(i):
-        side, to = ((1, mate_id), (0, sibling_id), (1, cross_id))[i]
-        return remote(tok.at[0, core], tok.at[side, core], ssem_c.at[i], rsem_c.at[i], to)
-
-    def come_c(i):
-        side, half, to = ((1, core, mate_id), (0, other, sibling_id), (1, other, cross_id))[i]
-        return remote(tok.at[0, core], tok.at[side, half], ssem_c.at[i], rsem_c.at[i], to)
-
-    for i in range(3):
-        send_c(i).start()
+    tok[core] = dot(settle, in_b[...].reshape(512, 128)).astype(BF16).reshape(2, TILES, 128)
+
+    send_c = remote(tok.at[core], tok.at[core], ssem_c, rsem_c, sibling_id)
+    come_c = remote(tok.at[core], tok.at[other], ssem_c, rsem_c, sibling_id)
+    send_c.start()
 
     project_text(1, tv)
+    spot_column = jnp.sum(landing[:, bit].reshape(256, TILES), axis=1, keepdims=True)
+    unsettle = onehot(spot_column == iota((256, TILES), 1).astype(F32) + 1.0)
     text_used = iota((TEXT_PAD, 128), 0) < TEXT
     for b in range(2):
         for s in range(SLABS):
@@ -262,18 +265,27 @@
 
     for load in (mod_load, wemb_load, q_load, k_load, v_load):
         load.wait()
-    for i in range(3):
-        come_c(i).wait_recv()
+    come_c.wait_recv()
     mod_copy.wait_recv()
 
-    def embed(side, half, source):
-        for low in range(2):
-            piece = tok[side, half][:, low * CH:(low + 1) * CH]
-            hidden = dot(piece, wemb[...])
+    for side in range(2):
+        for j in range(TILE):
+            line[side, j * TILES:(j + 1) * TILES, :] = (
+                tok[j // 2, side][:, (j % 2) * CH:(j % 2 + 1) * CH]
+            )
+
+    def embed(side):
+        for start in range(0, D, 256):
+            lanes = slice(start, min(start + 256, D))
+            hid[side, :, lanes] = dot(line[side], wemb[:, lanes])
+
+    def norm(side, half, source):
+        for i in range(2):
+            rows = pl.ds(pl.multiple_of(half * HALF + i * TILES, 32), TILES)
+            hidden = hid[side, rows, :]
             centred = hidden - jnp.mean(hidden, axis=-1, keepdims=True)
             spread = jnp.mean(centred * centred, axis=-1, keepdims=True)
             scaled = centred * lax.rsqrt(spread + EPS)
-            rows = pl.ds(pl.multiple_of((2 * half + low) * TILES, 32), TILES)
             for b in range(2):
                 normed[2 * side + b, rows, :] = (
                     scaled * (1.0 + source[1, b:b + 1, :]) + source[0, b:b + 1, :]
@@ -300,14 +312,17 @@
             for t, slab_index in enumerate(pair):
                 put(side, b, slab_index, out[:, t * 128:(t + 1) * 128])
 
+    embed(0)
+    embed(1)
+
     @pl.loop(0, 2)
     def _(half):
-        embed(0, half, mod)
+        norm(0, half, mod)
 
     @pl.loop(0, 2)
     def _(b):
         project(0, b, list(range(3 * SLABS)))
-        embed(1, b, mod_mate)
+        norm(1, b, mod_mate)
 
     @pl.loop(0, 2)
     def _(b):
@@ -330,13 +345,14 @@
                 rows, wout[:, start:start + size]
             ).astype(BF16)
 
-    lower = iota((ROWS, 128), 1) < HEAD
+    lower = iota((HALF, 128), 1) < HEAD
     wout_load.wait()
-
-    @pl.loop(0, 2)
-    def _(b):
+    wfin_load.wait()
+
+    def attend(b, half):
+        rows = pl.ds(pl.multiple_of(half * HALF, HALF), HALF)
         for s in range(SLABS):
-            query, key, value = qbuf[b, s], kbuf[b, s], vbuf[b, s]
+            query, key, value = qbuf[b, s, rows, :], kbuf[b, s], vbuf[b, s]
             parts = []
             for head in (lower, ~lower):
                 scores = lax.dot_general(
@@ -347,19 +363,18 @@
                 raised = jnp.exp2((scores - highest) * (HEAD ** (-0.5) * LOG2E)).astype(BF16)
                 both = dot(raised, value)
                 parts.append(both[:, :128] / both[:, 128:])
-            att[b, :, s * 128:(s + 1) * 128] = jnp.where(lower, parts[0], parts[1]).astype(BF16)
+            att[b, rows, s * 128:(s + 1) * 128] = jnp.where(lower, parts[0], parts[1]).astype(BF16)
+
+    @pl.loop(0, 2)
+    def _(b):
+        attend(b, other)
         project_out(b, other, 0)
         exchange(b).start()
 
-    wfin_load.wait()
-    for b in range(2):
+    @pl.loop(0, 2)
+    def _(b):
+        attend(b, core)
         project_out(b, core, 1)
-    for low in range(2):
-        piece = tok[0, core][:, low * CH:(low + 1) * CH]
-        for start, size in CHUNKS:
-            hid[low * TILES:(low + 1) * TILES, start:start + size] = dot(
-                piece, wemb[:, start:start + size]
-            )
 
     block = 48
     for b in range(2):
@@ -371,7 +386,8 @@
             rows = pl.ds(pl.multiple_of(i * block, block), block)
             kept = normed[1, pl.ds(pl.multiple_of(b * HALF + i * block, block), block), :]
             mixed = kept.astype(F32) + got[b, rows, :].astype(F32)
-            state = hid[rows, :] + gate * mixed
+            mine = pl.ds(pl.multiple_of(core * HALF + i * block, block), block)
+            state = hid[0, mine, :] + gate * mixed
             centred = state - jnp.mean(state, axis=-1, keepdims=True)
             spread = jnp.mean(centred * centred, axis=-1, keepdims=True)
             final = (centred * lax.rsqrt(spread + EPS) * (1.0 + scale) + shift).astype(BF16)
@@ -383,7 +399,6 @@
     position = (row - upper * TILES) * TILE + 2 * core + upper
     change = jnp.where(position < own_len, STEP * guided, 0.0)
     change = jnp.concatenate([change[:TILES], change[TILES:]], axis=1).astype(BF16)
-    unsettle = onehot(spot_column == iota((256, TILES), 1).astype(F32) + 1.0)
     home_b[...] = dot(unsettle, change).astype(BF16).reshape(XY, 16, 128)
 
     def return_b(k):
@@ -434,8 +449,7 @@
         send_b(k).wait_send()
         return_b(k).wait_send()
 
-    for i in range(3):
-        send_c(i).wait_send()
+    send_c.wait_send()
     mod_copy.wait_send()
     for b in range(2):
         exchange(b).wait_send()
@@ -467,6 +481,7 @@
             pltpu.VMEM((Z * XY, TILES), jnp.int32),
             pltpu.VMEM((5, 2, D), F32),
             pltpu.VMEM((2, 2, D), F32),
+            pltpu.VMEM((3, HEAD), F32),
             pltpu.VMEM((3, 128), F32),
             pltpu.VMEM((TEXT_PAD, 2, D), BF16),
             pltpu.VMEM((2 * TEXT_PAD, D), BF16),
@@ -485,11 +500,13 @@
             pltpu.VMEM((2, SLABS, KEYS, 256), BF16),
             pltpu.VMEM((2, ROWS, WIDTH), BF16),
             pltpu.VMEM((2, HALF, D), BF16),
-            pltpu.VMEM((HALF, D), F32),
+            pltpu.VMEM((2, ROWS, D), F32),
+            pltpu.VMEM((2, ROWS, CH), BF16),
             pltpu.VMEM((2, HALF, CH), F32),
-            narrow, narrow, wide, wide, wide, wide, narrow, narrow,
+            pltpu.VMEM((XY, 2, 16, TILES), F32),
+            narrow, narrow, narrow, pltpu.VMEM((XY, 32, 128), BF16), wide, wide, narrow, narrow,
             dma((12,)), dma((2,)), dma((Z,)), dma((Z,)), dma((XY,)), dma((XY,)),
-            dma((3,)), dma((3,)), dma((2,)), dma((2,)),
+            dma, dma, dma((2,)), dma((2,)),
             dma((XY,)), dma((XY,)), dma((Z,)), dma((Z,)),
         ],
         compiler_params=pltpu.CompilerParams(
@@ -505,7 +522,7 @@
 ):
     return step(
         latents, tile_slot.reshape(TILES, 128), modulation[0].transpose(1, 0, 2),
-        jnp.concatenate([norm_gains, norm_gains], axis=1), text_states[0].transpose(1, 0, 2),
+        norm_gains, text_states[0].transpose(1, 0, 2),
         w_text_kv, w_embed, w_qkv.transpose(1, 0, 2), w_out, w_final.T, live, partner,
     )
 

time: 76 us -> 74.7 us (0.983)
  other arithmetic: 1.41 us -> 0 us
    concatenate x1 -> x0, other arithmetic: 1.41 us -> none  [shards(): jnp.concatenate([norm_gains, norm_gains], axis=1)]
where the time goes in v4:
time: 74.7 us; the launch traced here: 73.8 us
  Pallas kernels  72.3 us (97%)
  local copies, waits for them, and re-layouts  1.42 us (2%)
    pallas_call x1, Pallas kernels, step(): pl.pallas_call(step_kernel, out_shape=jax.ShapeDtypeStruct((TILES, 128),...  72.3 us

profile of v4, /device:TPU:1, one launch (start us, length us, event | category | flops | bytes accessed | tf_op | source)
XLA Modules:
  0.0 73.8 jit_solution(3389113523737531597)
XLA Ops:
  0.0 72.3 %step.1 = f32[96,128]{1,0:T(8,128)} custom-call(f32[96,128]{1,0:T(8,128)} %lat_hbm.1, s32[96,128]{1,0:T(8,128)} %bitcast.13, f32[5,2,2432]{2,1,0:T(2,128)} %bitcast.12, f32[3,64]{1,0:T(4,128)} %gain_hbm.1, bf16[154,2,2432]{2,1,0:T(2,128)(2,1)} %bitcast.10, bf16[2432,2,640]{2,1,0:T(2,128)(2,1)} %wtext_hbm.1, bf16[64,2432]{1,0:T(8,128)(2,1)} %wemb_hbm.1, ...), custom_call_target="tpu_custom_call" | custom-call | tf_op jit(solution)/shard_map/step/pallas_call | solution.py:473
  72.4 1.4 %copy.14 = f32[96,128]{1,0:T(8,128)} copy(f32[96,128]{1,0:T(8,128)} %step.1) | data formatting | bytes 98304

commit v5 on v4

--- a/solution.py
+++ b/solution.py
@@ -59,7 +59,7 @@
 def step_kernel(
     lat_hbm, slot_hbm, mod_hbm, gain_hbm, text_hbm, wtext_hbm, wemb_hbm, wqkv_hbm, wout_hbm,
     wfin_hbm, live_ref, partner_ref, out_ref,
-    lat, slot_raw, slot_tab, mod, mod_mate, gain_half, gain, text_pairs, text, w_pairs, w_split, wemb, wqkv,
+    lat, slot_raw, slot_tab, mod, mod_mate, gain_half, gain, text_pairs, w_pairs, w_split, wemb, wqkv,
     wout, wfin, tk, tv, tok, normed, qbuf, kbuf, vbuf, att, got, hid, line, vel, landing,
     out_a, in_a, out_b, in_b, home_b, back_b, home_a, back_a,
     lsem, msem, ssem_a, rsem_a, ssem_b, rsem_b, ssem_c, rsem_c, xsend, xrecv,
@@ -165,33 +165,6 @@
         w_split[0, rows, :] = both[:128].astype(BF16)
         w_split[1, rows, :] = both[128:].astype(BF16)
 
-    row, col = iota((256, 256), 0), iota((256, 256), 1)
-    reorder = onehot(col == (row & 7) * 32 + (row >> 4) * 2 + ((row >> 3) & 1))
-
-    @pl.loop(1, Z)
-    def _(k):
-        come_a(k).wait_recv()
-
-    out_b[...] = dot(reorder, in_a[...].reshape(256, 128)).astype(BF16).reshape(XY // 2, 32, 128)
-
-    def send_b(k):
-        return remote(
-            out_b.at[lax.div(plane_peer(k), 2)], in_b.at[xy], ssem_b.at[k], rsem_b.at[xy],
-            plane_id(k),
-        )
-
-    def come_b(k):
-        at = plane_peer(k)
-        return remote(
-            out_b.at[lax.div(at, 2)], in_b.at[at], ssem_b.at[k], rsem_b.at[at], plane_id(k)
-        )
-
-    @pl.loop(1, XY)
-    def _(k):
-        send_b(k).start()
-
-    in_b[xy] = out_b[lax.div(xy, 2)]
-
     slot = slot_tab[...]
     target = group_of(slot)
     placed = slot - target * TILES
@@ -214,18 +187,46 @@
     )[:1]
     hit = iota((TILES, 512), 0).astype(F32) + 1.0 == spot_row
     member = (iota((TILES, 512), 1) >> 4) & 1
+    spot_column = jnp.sum(landing[:, bit].reshape(256, TILES), axis=1, keepdims=True)
+    unsettle = onehot(spot_column == iota((256, TILES), 1).astype(F32) + 1.0)
     settle = jnp.concatenate([onehot(hit & (member == bit)), onehot(hit & (member != bit))], axis=0)
+
+    row, col = iota((256, 256), 0), iota((256, 256), 1)
+    reorder = onehot(col == (row & 7) * 32 + (row >> 4) * 2 + ((row >> 3) & 1))
+
+    @pl.loop(1, Z)
+    def _(k):
+        come_a(k).wait_recv()
+
+    out_b[...] = dot(reorder, in_a[...].reshape(256, 128)).astype(BF16).reshape(XY // 2, 32, 128)
+
+    def send_b(k):
+        return remote(
+            out_b.at[lax.div(plane_peer(k), 2)], in_b.at[xy], ssem_b.at[k], rsem_b.at[xy],
+            plane_id(k),
+        )
+
+    def come_b(k):
+        at = plane_peer(k)
+        return remote(
+            out_b.at[lax.div(at, 2)], in_b.at[at], ssem_b.at[k], rsem_b.at[at], plane_id(k)
+        )
+
+    @pl.loop(1, XY)
+    def _(k):
+        send_b(k).start()
+
+    in_b[xy] = out_b[lax.div(xy, 2)]
 
     text_load.wait()
     gain_load.wait()
     gain[...] = jnp.concatenate([gain_half[...], gain_half[...]], axis=1)
-    text[...] = text_pairs[...].reshape(2 * TEXT_PAD, D)
     text_row, text_col = (iota((2 * TEXT_PAD, 2 * TEXT_PAD), i) for i in range(2))
     branch = jnp.where(text_row >= TEXT_PAD, 1, 0)
     part_text = onehot(text_col == (text_row - branch * TEXT_PAD) * 2 + branch)
 
     def project_text(c, out):
-        projected = dot(text[...], w_split[c])
+        projected = dot(text_pairs[...].reshape(2 * TEXT_PAD, D), w_split[c])
         if c == 0:
             slabs = [
                 head_norm(projected[:, i * 128:(i + 1) * 128], gain[2:3, :]) for i in range(SLABS)
@@ -234,20 +235,7 @@
         out[...] = dot(part_text, projected.astype(BF16)).astype(BF16).reshape(2, TEXT_PAD, WIDTH)
 
     project_text(0, tk)
-
-    @pl.loop(1, XY)
-    def _(k):
-        come_b(k).wait_recv()
-
-    tok[core] = dot(settle, in_b[...].reshape(512, 128)).astype(BF16).reshape(2, TILES, 128)
-
-    send_c = remote(tok.at[core], tok.at[core], ssem_c, rsem_c, sibling_id)
-    come_c = remote(tok.at[core], tok.at[other], ssem_c, rsem_c, sibling_id)
-    send_c.start()
-
     project_text(1, tv)
-    spot_column = jnp.sum(landing[:, bit].reshape(256, TILES), axis=1, keepdims=True)
-    unsettle = onehot(spot_column == iota((256, TILES), 1).astype(F32) + 1.0)
     text_used = iota((TEXT_PAD, 128), 0) < TEXT
     for b in range(2):
         for s in range(SLABS):
@@ -257,6 +245,17 @@
             vbuf[b, s, 2 * ROWS:, :128] = tv[b, :, lanes]
             vbuf[b, s, 2 * ROWS:, 128:] = onehot(text_used)
 
+
+    @pl.loop(1, XY)
+    def _(k):
+        come_b(k).wait_recv()
+
+    tok[core] = dot(settle, in_b[...].reshape(512, 128)).astype(BF16).reshape(2, TILES, 128)
+
+    send_c = remote(tok.at[core], tok.at[core], ssem_c, rsem_c, sibling_id)
+    come_c = remote(tok.at[core], tok.at[other], ssem_c, rsem_c, sibling_id)
+    send_c.start()
+
     own_len = live_ref[group]
     mate_len = jnp.where(partner_ref[group] != group, live_ref[mate], 0)
     row = iota((ROWS, 128), 0)
@@ -281,7 +280,7 @@
 
     def norm(side, half, source):
         for i in range(2):
-            rows = pl.ds(pl.multiple_of(half * HALF + i * TILES, 32), TILES)
+            rows = pl.ds(half * HALF + i * TILES if isinstance(half, int) else pl.multiple_of(half * HALF + i * TILES, 32), TILES)
             hidden = hid[side, rows, :]
             centred = hidden - jnp.mean(hidden, axis=-1, keepdims=True)
             spread = jnp.mean(centred * centred, axis=-1, keepdims=True)
@@ -313,19 +312,18 @@
                 put(side, b, slab_index, out[:, t * 128:(t + 1) * 128])
 
     embed(0)
-    embed(1)
 
     @pl.loop(0, 2)
     def _(half):
         norm(0, half, mod)
 
-    @pl.loop(0, 2)
-    def _(b):
+    embed(1)
+
+    for b in range(2):
+        norm(1, b, mod_mate)
         project(0, b, list(range(3 * SLABS)))
-        norm(1, b, mod_mate)
-
-    @pl.loop(0, 2)
-    def _(b):
+
+    for b in range(2):
         project(1, b, list(range(SLABS, 3 * SLABS)))
 
     def half_rows(b):
@@ -345,14 +343,13 @@
                 rows, wout[:, start:start + size]
             ).astype(BF16)
 
-    lower = iota((HALF, 128), 1) < HEAD
+    lower = iota((ROWS, 128), 1) < HEAD
     wout_load.wait()
     wfin_load.wait()
 
-    def attend(b, half):
-        rows = pl.ds(pl.multiple_of(half * HALF, HALF), HALF)
+    def attend(b):
         for s in range(SLABS):
-            query, key, value = qbuf[b, s, rows, :], kbuf[b, s], vbuf[b, s]
+            query, key, value = qbuf[b, s], kbuf[b, s], vbuf[b, s]
             parts = []
             for head in (lower, ~lower):
                 scores = lax.dot_general(
@@ -363,17 +360,15 @@
                 raised = jnp.exp2((scores - highest) * (HEAD ** (-0.5) * LOG2E)).astype(BF16)
                 both = dot(raised, value)
                 parts.append(both[:, :128] / both[:, 128:])
-            att[b, rows, s * 128:(s + 1) * 128] = jnp.where(lower, parts[0], parts[1]).astype(BF16)
+            att[b, :, s * 128:(s + 1) * 128] = jnp.where(lower, parts[0], parts[1]).astype(BF16)
 
     @pl.loop(0, 2)
     def _(b):
-        attend(b, other)
+        attend(b)
         project_out(b, other, 0)
         exchange(b).start()
 
-    @pl.loop(0, 2)
-    def _(b):
-        attend(b, core)
+    for b in range(2):
         project_out(b, core, 1)
 
     block = 48
@@ -484,7 +479,6 @@
             pltpu.VMEM((3, HEAD), F32),
             pltpu.VMEM((3, 128), F32),
             pltpu.VMEM((TEXT_PAD, 2, D), BF16),
-            pltpu.VMEM((2 * TEXT_PAD, D), BF16),
             pltpu.VMEM((D, 2, WIDTH), BF16),
             pltpu.VMEM((2, D, WIDTH), BF16),
             pltpu.VMEM((CH, D), BF16),
@@ -510,7 +504,7 @@
             dma((XY,)), dma((XY,)), dma((Z,)), dma((Z,)),
         ],
         compiler_params=pltpu.CompilerParams(
-            collective_id=0, has_side_effects=True, vmem_limit_bytes=62 << 20
+            collective_id=0, has_side_effects=True, vmem_limit_bytes=63 << 20
         ),
         name="step",
     )(*operands)

time: 74.7 us -> 72.5 us (0.971); the launches traced: 73.8 us -> 72.4 us
  Pallas kernels: 72.3 us -> 71 us
    pallas_call x1, Pallas kernels: 72.3 us -> 71 us  [step(): pl.pallas_call(step_kernel, out_shape=jax.ShapeDtypeStruct((TILES, 128),...]
where the time goes in v5:
time: 72.5 us; the launch traced here: 72.4 us
  Pallas kernels  71 us (98%)
  local copies, waits for them, and re-layouts  1.42 us (2%)
    pallas_call x1, Pallas kernels, step(): pl.pallas_call(step_kernel, out_shape=jax.ShapeDtypeStruct((TILES, 128),...  71 us

profile of v5, /device:TPU:1, one launch (start us, length us, event | category | flops | bytes accessed | tf_op | source)
XLA Modules:
  0.0 72.4 jit_solution(16584552145799965685)
XLA Ops:
  0.0 71.0 %step.1 = f32[96,128]{1,0:T(8,128)} custom-call(f32[96,128]{1,0:T(8,128)} %lat_hbm.1, s32[96,128]{1,0:T(8,128)} %bitcast.13, f32[5,2,2432]{2,1,0:T(2,128)} %bitcast.12, f32[3,64]{1,0:T(4,128)} %gain_hbm.1, bf16[154,2,2432]{2,1,0:T(2,128)(2,1)} %bitcast.10, bf16[2432,2,640]{2,1,0:T(2,128)(2,1)} %wtext_hbm.1, bf16[64,2432]{1,0:T(8,128)(2,1)} %wemb_hbm.1, ...), custom_call_target="tpu_custom_call" | custom-call | tf_op jit(solution)/shard_map/step/pallas_call | solution.py:468
  71.0 1.4 %copy.14 = f32[96,128]{1,0:T(8,128)} copy(f32[96,128]{1,0:T(8,128)} %step.1) | data formatting | bytes 98304

commit v6 on v5

--- a/solution.py
+++ b/solution.py
@@ -60,7 +60,7 @@
     lat_hbm, slot_hbm, mod_hbm, gain_hbm, text_hbm, wtext_hbm, wemb_hbm, wqkv_hbm, wout_hbm,
     wfin_hbm, live_ref, partner_ref, out_ref,
     lat, slot_raw, slot_tab, mod, mod_mate, gain_half, gain, text_pairs, w_pairs, w_split, wemb, wqkv,
-    wout, wfin, tk, tv, tok, normed, qbuf, kbuf, vbuf, att, got, hid, line, vel, landing,
+    wout, wfin, tk, tv, tok, normed, qbuf, kbuf, vbuf, att, got, hid, line, landing,
     out_a, in_a, out_b, in_b, home_b, back_b, home_a, back_a,
     lsem, msem, ssem_a, rsem_a, ssem_b, rsem_b, ssem_c, rsem_c, xsend, xrecv,
     hsend_b, hrecv_b, hsend_a, hrecv_a,
@@ -371,7 +371,7 @@
     for b in range(2):
         project_out(b, core, 1)
 
-    block = 48
+    block = 96
     for b in range(2):
         exchange(b).wait_recv()
         gate, shift, scale = (mod[i, b:b + 1, :] for i in (2, 3, 4))
@@ -386,9 +386,10 @@
             centred = state - jnp.mean(state, axis=-1, keepdims=True)
             spread = jnp.mean(centred * centred, axis=-1, keepdims=True)
             final = (centred * lax.rsqrt(spread + EPS) * (1.0 + scale) + shift).astype(BF16)
-            vel[b, rows, :] = lax.dot_general(final, wfin[...], NT, preferred_element_type=F32)
-
-    guided = vel[1] + GUIDE * (vel[0] - vel[1])
+            normed[2, pl.ds(pl.multiple_of(b * HALF + i * block, block), block), :] = final
+
+    velocity = lax.dot_general(normed[2], wfin[...], NT, preferred_element_type=F32)
+    guided = velocity[HALF:] + GUIDE * (velocity[:HALF] - velocity[HALF:])
     row = iota((HALF, CH), 0)
     upper = jnp.where(row >= TILES, 1, 0)
     position = (row - upper * TILES) * TILE + 2 * core + upper
@@ -496,7 +497,6 @@
             pltpu.VMEM((2, HALF, D), BF16),
             pltpu.VMEM((2, ROWS, D), F32),
             pltpu.VMEM((2, ROWS, CH), BF16),
-            pltpu.VMEM((2, HALF, CH), F32),
             pltpu.VMEM((XY, 2, 16, TILES), F32),
             narrow, narrow, narrow, pltpu.VMEM((XY, 32, 128), BF16), wide, wide, narrow, narrow,
             dma((12,)), dma((2,)), dma((Z,)), dma((Z,)), dma((XY,)), dma((XY,)),

time: 72.5 us -> 71.2 us (0.982)
  Pallas kernels: 71 us -> 69.7 us
    pallas_call x1, Pallas kernels: 71 us -> 69.7 us  [step(): pl.pallas_call(step_kernel, out_shape=jax.ShapeDtypeStruct((TILES, 128),...]
where the time goes in v6:
time: 71.2 us; the launch traced here: 71.1 us
  Pallas kernels  69.7 us (98%)
  local copies, waits for them, and re-layouts  1.42 us (2%)
    pallas_call x1, Pallas kernels, step(): pl.pallas_call(step_kernel, out_shape=jax.ShapeDtypeStruct((TILES, 128),...  69.7 us

profile of v6, /device:TPU:1, one launch (start us, length us, event | category | flops | bytes accessed | tf_op | source)
XLA Modules:
  0.0 71.1 jit_solution(8649571399916878896)
XLA Ops:
  0.0 69.7 %step.1 = f32[96,128]{1,0:T(8,128)} custom-call(f32[96,128]{1,0:T(8,128)} %lat_hbm.1, s32[96,128]{1,0:T(8,128)} %bitcast.13, f32[5,2,2432]{2,1,0:T(2,128)} %bitcast.12, f32[3,64]{1,0:T(4,128)} %gain_hbm.1, bf16[154,2,2432]{2,1,0:T(2,128)(2,1)} %bitcast.10, bf16[2432,2,640]{2,1,0:T(2,128)(2,1)} %wtext_hbm.1, bf16[64,2432]{1,0:T(8,128)(2,1)} %wemb_hbm.1, ...), custom_call_target="tpu_custom_call" | custom-call | tf_op jit(solution)/shard_map/step/pallas_call | solution.py:469
  69.7 1.4 %copy.14 = f32[96,128]{1,0:T(8,128)} copy(f32[96,128]{1,0:T(8,128)} %step.1) | data formatting | bytes 98304
